TPU v7x, 512 devices: a whole 4x4x16 slice. The times are simulated.
512 devices in a mesh: seq: 32 (over x, z_lo), head: 16 (over y, z_hi, core).
Axes of the slice: x: 4, y: 4, z: 16 (z_hi: 2, z_lo: 8; z = z_hi * 8 + z_lo), core: 2. Of those that a mesh axis runs over, the one named last changes fastest.
Arguments:
- queries: bfloat16 [32, 16384, 128], P('head', 'seq'), may hold values from -30 to 30
- key_tokens: bfloat16 [16, 16384, 128], P('head', 'seq'), may hold values from -12 to 12
- value_tokens: bfloat16 [16, 16384, 128], P('head', 'seq'), may hold values from -6 to 6
- output_gradient: bfloat16 [32, 16384, 128], P('head', 'seq'), may hold values from -144 to 144
- summary_proj: bfloat16 [256, 16384], P(None, 'seq'), may hold values from -0.046875 to 0.046875
- partner_bits: int32 [32, 4], P('seq'), may hold values from 0 to 4, all different within a row
Outputs:
- attention_out: bfloat16 [32, 16384, 128], P('head', 'seq')
- query_grad: bfloat16 [32, 16384, 128], P('head', 'seq')
- key_grad: bfloat16 [16, 16384, 128], P('head', 'seq')
- value_grad: bfloat16 [16, 16384, 128], P('head', 'seq')
- proj_grad: float32 [256, 16384], P('head', 'seq')
Inputs may be any that keep to these rules, and one draw needn't show every extreme that they name: `partner_bits`: each row names 4 different bit positions.
All inputs are finite; a program needn't handle non-finite values.
Results may differ from a plain program's by a relative error of at most 0.025.
Values may be sent and summed in bfloat16 or wider, within the bound.
A program may use at most 64 MiB of HBM per device.

v0:
```python
import jax
import jax.numpy as jnp
from jax import lax
from jax.sharding import PartitionSpec as P

QUERY_HEADS = 32
KEY_VALUE_HEADS = 16
BLOCK = 512
PARTNERS = 4


score_scale = 1.0 / 12.0
highest = lax.Precision.HIGHEST


def from_partner(value, axis, apart):
    mask = 2**apart
    pairs = [(source, source ^ mask) for source in range(lax.axis_size(axis))]
    return lax.ppermute(value, axis, pairs)


def split_up(x, dim, size):
    before, after = (x.shape[:dim], x.shape[dim + 1 :])
    return jnp.moveaxis(x.reshape(*before, size, -1, *after), dim, 0)


def summed_on_arrival(x, axis, dim):
    size = lax.axis_size(axis)
    tiles = lax.all_to_all(split_up(x, dim, size), axis, 0, 0, tiled=True)
    return jnp.sum(tiles, axis=0)


def rows_for(lines, size):
    spare = -len(lines) % size
    return jnp.pad(lines, [(0, spare)] + [(0, 0)] * (lines.ndim - 1))


def joined_along(tiles, dim):
    shape = list(tiles.shape[1:])
    shape[dim] *= tiles.shape[0]
    return jnp.moveaxis(tiles, 0, dim).reshape(shape)


def copy_for_each(x, axis):
    copies = jnp.broadcast_to(x, (lax.axis_size(axis), *x.shape))
    return lax.all_to_all(copies, axis, split_axis=0, concat_axis=0, tiled=True)


def collect(x, axis, dim):
    return joined_along(copy_for_each(x, axis), dim)


def total_of(x, axes):
    own = summed_on_arrival(rows_for(x, lax.axis_size(axes)), axes, 0)
    whole = collect(own, axes, 0)
    return whole[: len(x)].reshape(x.shape)


def in_one(arrays, axis):
    ends = [0]
    for a in arrays:
        ends.append(ends[-1] + a.size)
    running = total_of(jnp.concatenate([a.ravel() for a in arrays]), axis)
    return tuple((running[b:e].reshape(a.shape) for a, b, e in zip(arrays, ends, ends[1:])))


def sent_and_summed(x, axis, dim):
    tiles = split_up(x, dim, lax.axis_size(axis))
    arrived = lax.all_to_all(tiles, axis, split_axis=0, concat_axis=0, tiled=True)
    return arrived.astype(jnp.float32).sum(axis=0)


def nested_sum(x, axes):
    lines = x.reshape(-1, x.shape[-1])
    own = sent_and_summed(rows_for(lines, lax.axis_size(axes)), axes, 0)
    whole = collect(own.astype(jnp.bfloat16), axes, 0)
    return whole[: len(lines)].reshape(x.shape).astype(jnp.float32)


def fetch_partners(key_blocks, value_blocks, visit_order, local_bits):
    fetched = [None] * len(visit_order)
    for bit_index in visit_order:
        fetched[bit_index] = from_partner((key_blocks, value_blocks), "seq", bit_index - local_bits)
    return fetched


def select_partners(fetched, partner_bits):
    chosen = []
    for slot_index in range(PARTNERS):
        bits_here = partner_bits[:, slot_index].reshape(1, -1, 1, 1)
        picked_keys = jnp.zeros_like(fetched[0][0])
        picked_values = jnp.zeros_like(fetched[0][1])
        for bit_index in range(len(fetched)):
            picked_keys = jnp.where(bits_here == bit_index, fetched[bit_index][0], picked_keys)
            picked_values = jnp.where(bits_here == bit_index, fetched[bit_index][1], picked_values)
        chosen.append((picked_keys, picked_values))
    return chosen


def pair_products(left_side, right_side):
    if right_side.ndim == 3:
        return jnp.einsum(
            "hgbqd,hkd->hgbqk", left_side, right_side, preferred_element_type=jnp.float32
        )
    return jnp.einsum(
        "hgbqd,hbkd->hgbqk", left_side, right_side, preferred_element_type=jnp.float32
    )


def mix_rows(weights, right_side):
    if right_side.ndim == 3:
        return jnp.einsum(
            "hgbqk,hkd->hgbqd", weights, right_side, preferred_element_type=jnp.float32
        )
    return jnp.einsum("hgbqk,hbkd->hgbqd", weights, right_side, preferred_element_type=jnp.float32)


def back_rows(weights, left_side, summary):
    if summary:
        return jnp.einsum(
            "hgbqk,hgbqd->hkd", weights, left_side, preferred_element_type=jnp.float32
        )
    return jnp.einsum("hgbqk,hgbqd->hbkd", weights, left_side, preferred_element_type=jnp.float32)


def per_device(queries, key_tokens, value_tokens, output_gradient, summary_proj, partner_bits):
    kv_heads = key_tokens.shape[0]
    head_dim = key_tokens.shape[2]
    blocks = key_tokens.shape[1] // BLOCK
    group_width = QUERY_HEADS // KEY_VALUE_HEADS
    local_bits = blocks.bit_length() - 1
    all_bits = local_bits + lax.axis_size("seq").bit_length() - 1
    visit_order = list(range(all_bits))
    block_shape = (kv_heads, blocks, BLOCK, head_dim)
    query_shape = (kv_heads, group_width, blocks, BLOCK, head_dim)
    key_blocks = key_tokens.reshape(block_shape)
    value_blocks = value_tokens.reshape(block_shape)
    query_blocks = queries.reshape(query_shape)
    grad_blocks = output_gradient.reshape(query_shape)
    partial_keys = jnp.einsum(
        "st,htd->hsd", summary_proj, key_tokens, preferred_element_type=jnp.float32
    )
    partial_values = jnp.einsum(
        "st,htd->hsd", summary_proj, value_tokens, preferred_element_type=jnp.float32
    )
    summed_keys, summed_values = in_one((partial_keys, partial_values), "seq")
    summary_pair = (summed_keys.astype(jnp.bfloat16), summed_values.astype(jnp.bfloat16))
    chosen = select_partners(
        fetch_partners(key_blocks, value_blocks, visit_order, local_bits), partner_bits
    )
    groups = [(key_blocks, value_blocks)] + chosen + [summary_pair]
    score_list = [
        pair_products(query_blocks, group_keys) * score_scale for group_keys, group_values in groups
    ]
    row_max = None
    for scores in score_list:
        local_max = jnp.max(scores, axis=-1, keepdims=True)
        row_max = local_max if row_max is None else jnp.maximum(row_max, local_max)
    row_total = jnp.zeros(row_max.shape, jnp.float32)
    mixed = jnp.zeros(query_shape, jnp.float32)
    exponents = []
    for scores, group_pair in zip(score_list, groups):
        exponent = jnp.exp(scores - row_max)
        exponents.append(exponent)
        row_total = row_total + jnp.sum(exponent, axis=-1, keepdims=True)
        mixed = mixed + mix_rows(exponent.astype(jnp.bfloat16), group_pair[1])
    attended = mixed / row_total
    attention_out = attended.astype(jnp.bfloat16).reshape(queries.shape)
    row_delta = jnp.sum(grad_blocks.astype(jnp.float32) * attended, axis=-1, keepdims=True)
    query_sum = jnp.zeros(query_shape, jnp.float32)
    pieces = []
    for position, group_pair in enumerate(groups):
        group_keys, group_values = group_pair
        is_summary = position == len(groups) - 1
        probabilities = exponents[position] / row_total
        prob_grad = pair_products(grad_blocks, group_values)
        grad_scores = (probabilities * (prob_grad - row_delta)).astype(jnp.bfloat16)
        query_sum = query_sum + mix_rows(grad_scores, group_keys)
        key_piece = back_rows(grad_scores, query_blocks, is_summary) * score_scale
        value_piece = back_rows(probabilities.astype(jnp.bfloat16), grad_blocks, is_summary)
        pieces.append((key_piece, value_piece))
    query_grad = (query_sum * score_scale).astype(jnp.bfloat16).reshape(queries.shape)
    summary_key_grads, summary_value_grads = (
        nested_sum(pieces[-1][0].astype(jnp.bfloat16), "seq"),
        nested_sum(pieces[-1][1].astype(jnp.bfloat16), "seq"),
    )
    proj_wide = summary_proj.astype(jnp.float32)
    key_total = pieces[0][0] + jnp.einsum(
        "st,hsd->htd", proj_wide, summary_key_grads, precision=highest
    ).reshape(block_shape)
    value_total = pieces[0][1] + jnp.einsum(
        "st,hsd->htd", proj_wide, summary_value_grads, precision=highest
    ).reshape(block_shape)
    low_keys = [pieces[1 + slot_index][0].astype(jnp.bfloat16) for slot_index in range(PARTNERS)]
    low_values = [pieces[1 + slot_index][1].astype(jnp.bfloat16) for slot_index in range(PARTNERS)]
    for bit_index in visit_order:
        send_keys = jnp.zeros(block_shape, jnp.bfloat16)
        send_values = jnp.zeros(block_shape, jnp.bfloat16)
        for slot_index in range(PARTNERS):
            bits_here = partner_bits[:, slot_index].reshape(1, -1, 1, 1) == bit_index
            send_keys = jnp.where(bits_here, low_keys[slot_index], send_keys)
            send_values = jnp.where(bits_here, low_values[slot_index], send_values)
        returned = from_partner((send_keys, send_values), "seq", bit_index - local_bits)
        key_total = key_total + returned[0].astype(jnp.float32)
        value_total = value_total + returned[1].astype(jnp.float32)
    key_grad = key_total.astype(jnp.bfloat16).reshape(key_tokens.shape)
    value_grad = value_total.astype(jnp.bfloat16).reshape(value_tokens.shape)
    keys_wide = key_tokens.astype(jnp.float32)
    values_wide = value_tokens.astype(jnp.float32)
    key_term = jnp.einsum("hsd,htd->st", summary_key_grads, keys_wide, precision=highest)
    value_term = jnp.einsum("hsd,htd->st", summary_value_grads, values_wide, precision=highest)
    proj_grad = sent_and_summed((key_term + value_term).astype(jnp.bfloat16), "head", 0)
    return (attention_out, query_grad, key_grad, value_grad, proj_grad)


def solution(mesh):
    in_specs = (
        P("head", "seq", None),
        P("head", "seq", None),
        P("head", "seq", None),
        P("head", "seq", None),
        P(None, "seq"),
        P("seq", None),
    )
    out_specs = (
        P("head", "seq", None),
        P("head", "seq", None),
        P("head", "seq", None),
        P("head", "seq", None),
        P("head", "seq"),
    )
    return jax.shard_map(
        per_device, mesh=mesh, in_specs=in_specs, out_specs=out_specs, check_vma=False
    )
```

profile of v0, /device:TPU:1, one launch (start us, length us, event | category | flops | bytes accessed | tf_op | source)
XLA Modules:
  0.0 279.2 jit_solution(733767044775659127)
XLA Ops:
  0.7 5.6 %collective-permute-start = (bf16[1,1,512,128]{3,2,1,0:T(8,128)(2,1)}, bf16[1,1,512,128]{3,2,1,0:T(8,128)(2,1)S(1)}, u32[]{:S(2)}, u32[]{:S(2)}) collective-permute-start(bf16[1,1,512,128]{3,2,1,0:T(8,128)(2,1)} %bitcast.565), channel_id=1, source_target_pairs={{0,256},{16,272},{32,288},{48,304},{64,320},{80,336},{96,352},{112... | collective-permute-start | bytes 393224 | tf_op jit(solution)/shard_map/ppermute | solution.py:19
  6.3 2.2 collective-permute-start.1
  8.5 8.8 %collective-permute-start.2 = (bf16[1,1,512,128]{3,2,1,0:T(8,128)(2,1)}, bf16[1,1,512,128]{3,2,1,0:T(8,128)(2,1)}, u32[]{:S(2)}, u32[]{:S(2)}) collective-permute-start(bf16[1,1,512,128]{3,2,1,0:T(8,128)(2,1)} %bitcast.567), channel_id=1, source_target_pairs={{0,64},{16,80},{32,96},{48,112},{64,0},{80,16},{96,32},{112,48},{1... | collective-permute-start | bytes 393224 | tf_op jit(solution)/shard_map/ppermute | solution.py:19
  17.3 4.9 %collective-permute-start.3 = (bf16[1,1,512,128]{3,2,1,0:T(8,128)(2,1)}, bf16[1,1,512,128]{3,2,1,0:T(8,128)(2,1)}, u32[]{:S(2)}, u32[]{:S(2)}) collective-permute-start(bf16[1,1,512,128]{3,2,1,0:T(8,128)(2,1)} %bitcast.568), channel_id=1, source_target_pairs={{0,32},{16,48},{32,0},{48,16},{64,96},{80,112},{96,64},{112,80},{1... | collective-permute-start | bytes 393224 | tf_op jit(solution)/shard_map/ppermute | solution.py:19
  22.2 3.5 %collective-permute-start.4 = (bf16[1,1,512,128]{3,2,1,0:T(8,128)(2,1)}, bf16[1,1,512,128]{3,2,1,0:T(8,128)(2,1)}, u32[]{:S(2)}, u32[]{:S(2)}) collective-permute-start(bf16[1,1,512,128]{3,2,1,0:T(8,128)(2,1)} %bitcast.569), channel_id=1, source_target_pairs={{0,16},{16,0},{32,48},{48,32},{64,80},{80,64},{96,112},{112,96},{1... | collective-permute-start | bytes 393224 | tf_op jit(solution)/shard_map/ppermute | solution.py:19
  25.8 1.2 convolution_bitcast_fusion.19
  27.2 1.2 convolution_bitcast_fusion.18
  29.6 3.9 %all-to-all-start = ((f32[32,1,2048]{2,1,0:T(1,128)}), f32[32,1,2048]{2,1,0:T(1,128)S(1)}, u32[]{:S(2)}, u32[]{:S(2)}) async-start(f32[32,1,2048]{2,1,0:T(1,128)} %copy.108), calls=%async_computation | async-start | bytes 524288 | tf_op jit(solution)/shard_map/all_to_all | solution.py:29
  47.5 1.8 copy.121
  49.3 4.6 %collective-permute-start.5 = (bf16[1,1,512,128]{3,2,1,0:T(8,128)(2,1)S(1)}, bf16[1,1,512,128]{3,2,1,0:T(8,128)(2,1)S(1)}, u32[]{:S(2)}, u32[]{:S(2)}) collective-permute-start(bf16[1,1,512,128]{3,2,1,0:T(8,128)(2,1)S(1)} %bitcast.570), channel_id=1, source_target_pairs={{0,256},{16,272},{32,288},{48,304},{64,320},{80,336},{96,352},{112... | collective-permute-start | bytes 393224 | tf_op jit(solution)/shard_map/ppermute | solution.py:19
  53.9 2.2 collective-permute-start.6
  56.2 7.0 %collective-permute-start.7 = (bf16[1,1,512,128]{3,2,1,0:T(8,128)(2,1)S(1)}, bf16[1,1,512,128]{3,2,1,0:T(8,128)(2,1)S(1)}, u32[]{:S(2)}, u32[]{:S(2)}) collective-permute-start(bf16[1,1,512,128]{3,2,1,0:T(8,128)(2,1)S(1)} %bitcast.572), channel_id=1, source_target_pairs={{0,64},{16,80},{32,96},{48,112},{64,0},{80,16},{96,32},{112,48},{1... | collective-permute-start | bytes 393224 | tf_op jit(solution)/shard_map/ppermute | solution.py:19
  63.2 4.0 %collective-permute-start.8 = (bf16[1,1,512,128]{3,2,1,0:T(8,128)(2,1)S(1)}, bf16[1,1,512,128]{3,2,1,0:T(8,128)(2,1)S(1)}, u32[]{:S(2)}, u32[]{:S(2)}) collective-permute-start(bf16[1,1,512,128]{3,2,1,0:T(8,128)(2,1)S(1)} %bitcast.573), channel_id=1, source_target_pairs={{0,32},{16,48},{32,0},{48,16},{64,96},{80,112},{96,64},{112,80},{1... | collective-permute-start | bytes 393224 | tf_op jit(solution)/shard_map/ppermute | solution.py:19
  67.3 3.1 %collective-permute-start.9 = (bf16[1,1,512,128]{3,2,1,0:T(8,128)(2,1)S(1)}, bf16[1,1,512,128]{3,2,1,0:T(8,128)(2,1)S(1)}, u32[]{:S(2)}, u32[]{:S(2)}) collective-permute-start(bf16[1,1,512,128]{3,2,1,0:T(8,128)(2,1)S(1)} %bitcast.574), channel_id=1, source_target_pairs={{0,16},{16,0},{32,48},{48,32},{64,80},{80,64},{96,112},{112,96},{1... | collective-permute-start | bytes 393224 | tf_op jit(solution)/shard_map/ppermute | solution.py:19
  71.5 2.2 collective-permute-done.7
  73.7 1.8 collective-permute-done.8
  77.5 1.8 bitcast_reduce_fusion
  79.4 1.8 bitcast_reduce_fusion.1
  81.2 2.4 bitcast_reduce_fusion.2
  84.4 1.4 reduce.23
  86.5 11.3 %all-to-all-start.1 = ((bf16[32,2,1024]{2,1,0:T(2,128)(2,1)}), bf16[32,2,1024]{2,1,0:T(2,128)(2,1)S(1)}, u32[]{:S(2)}, u32[]{:S(2)}) async-start(bf16[32,2,1024]{2,1,0:T(2,128)(2,1)} %reshape.682), calls=%async_computation.1 | async-start | bytes 262144 | tf_op jit(solution)/shard_map/all_to_all | solution.py:46
  97.9 1.8 select_select_fusion.3
  99.7 2.4 bitcast_reduce_fusion.3
  102.1 7.5 %all-to-all-done.1 = bf16[32,2,1024]{2,1,0:T(2,128)(2,1)S(1)} async-done(((bf16[32,2,1024]{2,1,0:T(2,128)(2,1)}), bf16[32,2,1024]{2,1,0:T(2,128)(2,1)S(1)}, u32[]{:S(2)}, u32[]{:S(2)}) %all-to-all-start.1) | async-done | bytes 131104 | tf_op jit(solution)/shard_map/all_to_all | solution.py:46
  112.2 1.3 fusion.177
  114.5 1.4 convolution_bitcast_fusion.3
  116.0 4.1 %fusion.22 = (f32[2,512]{1,0:T(2,128)S(1)}, f32[2,512]{1,0:T(2,128)S(1)}, f32[2,512]{1,0:T(2,128)S(1)}, f32[2,512]{1,0:T(2,128)S(1)}, f32[2,512]{1,0:T(2,128)S(1)}) fusion(f32[512,2,512]{2,0,1:T(8,128)} %get-tuple-element.67, f32[2,512]{1,0:T(2,128)S(1)} %maximum_maximum_fusion, f32[512,2,512]{2,0,1:T(8,128)S(1)} %get-tuple-element.65, ...), kind=kLoop, calls=%fused_computation.44 | loop fusion | flops 7859200 | bytes 10510336 | tf_op jit(solution)/shard_map/reduce_sum | solution.py:165
  127.1 1.3 fusion.118
  128.4 1.6 fusion.11
  130.7 1.6 fusion.13
  132.3 1.6 fusion.14
  134.6 1.2 fusion.56
  135.7 1.5 convolution_bitcast_fusion.1
  137.2 1.1 fusion.64
  138.3 1.4 fusion.142
  140.9 1.1 convolution_bitcast_fusion
  142.1 6.9 %all-to-all-start.2 = ((bf16[32,8,128]{2,1,0:T(8,128)(2,1)}), bf16[32,8,128]{2,1,0:T(8,128)(2,1)}, u32[]{:S(2)}, u32[]{:S(2)}) async-start(bf16[32,8,128]{2,1,0:T(8,128)(2,1)} %fusion.70), calls=%async_computation.2 | async-start | bytes 131072 | tf_op jit(solution)/shard_map/all_to_all | solution.py:69
  149.0 4.1 %collective-permute-start.16 = (bf16[1,1,512,128]{3,2,1,0:T(8,128)(2,1)}, bf16[1,1,512,128]{3,2,1,0:T(8,128)(2,1)}, u32[]{:S(2)}, u32[]{:S(2)}) collective-permute-start(bf16[1,1,512,128]{3,2,1,0:T(8,128)(2,1)} %get-tuple-element.43), channel_id=1, source_target_pairs={{0,32},{16,48},{32,0},{48,16},{64,96},{80,112},{96,64},{112,80},{1... | collective-permute-start | bytes 393224 | tf_op jit(solution)/shard_map/ppermute | solution.py:19
  153.1 7.0 %collective-permute-start.17 = (bf16[1,1,512,128]{3,2,1,0:T(8,128)(2,1)}, bf16[1,1,512,128]{3,2,1,0:T(8,128)(2,1)}, u32[]{:S(2)}, u32[]{:S(2)}) collective-permute-start(bf16[1,1,512,128]{3,2,1,0:T(8,128)(2,1)} %get-tuple-element.44), channel_id=1, source_target_pairs={{0,64},{16,80},{32,96},{48,112},{64,0},{80,16},{96,32},{112,48},{1... | collective-permute-start | bytes 393224 | tf_op jit(solution)/shard_map/ppermute | solution.py:19
  160.1 3.1 %collective-permute-start.15 = (bf16[1,1,512,128]{3,2,1,0:T(8,128)(2,1)}, bf16[1,1,512,128]{3,2,1,0:T(8,128)(2,1)}, u32[]{:S(2)}, u32[]{:S(2)}) collective-permute-start(bf16[1,1,512,128]{3,2,1,0:T(8,128)(2,1)} %get-tuple-element.40), channel_id=1, source_target_pairs={{0,16},{16,0},{32,48},{48,32},{64,80},{80,64},{96,112},{112,96},{1... | collective-permute-start | bytes 393224 | tf_op jit(solution)/shard_map/ppermute | solution.py:19
  163.2 3.1 %collective-permute-start.18 = (bf16[1,1,512,128]{3,2,1,0:T(8,128)(2,1)}, bf16[1,1,512,128]{3,2,1,0:T(8,128)(2,1)}, u32[]{:S(2)}, u32[]{:S(2)}) collective-permute-start(bf16[1,1,512,128]{3,2,1,0:T(8,128)(2,1)} %get-tuple-element.42), channel_id=1, source_target_pairs={{0,128},{16,144},{32,160},{48,176},{64,192},{80,208},{96,224},{112... | collective-permute-start | bytes 393224 | tf_op jit(solution)/shard_map/ppermute | solution.py:19
  166.3 4.5 %collective-permute-start.19 = (bf16[1,1,512,128]{3,2,1,0:T(8,128)(2,1)}, bf16[1,1,512,128]{3,2,1,0:T(8,128)(2,1)}, u32[]{:S(2)}, u32[]{:S(2)}) collective-permute-start(bf16[1,1,512,128]{3,2,1,0:T(8,128)(2,1)} %get-tuple-element.41), channel_id=1, source_target_pairs={{0,256},{16,272},{32,288},{48,304},{64,320},{80,336},{96,352},{112... | collective-permute-start | bytes 393224 | tf_op jit(solution)/shard_map/ppermute | solution.py:19
  170.9 2.3 fusion.65
  173.2 1.9 fusion.138
  175.7 1.3 fusion.57
  177.9 4.0 %all-to-all-start.4 = ((bf16[32,8,128]{2,1,0:T(8,128)(2,1)}), bf16[32,8,128]{2,1,0:T(8,128)(2,1)S(1)}, u32[]{:S(2)}, u32[]{:S(2)}) async-start(bf16[32,8,128]{2,1,0:T(8,128)(2,1)} %fusion.69), calls=%async_computation.4 | async-start | bytes 131072 | tf_op jit(solution)/shard_map/all_to_all | solution.py:69
  181.9 1.7 fusion.63
  184.5 8.9 %all-to-all-done.4 = bf16[32,8,128]{2,1,0:T(8,128)(2,1)S(1)} async-done(((bf16[32,8,128]{2,1,0:T(8,128)(2,1)}), bf16[32,8,128]{2,1,0:T(8,128)(2,1)S(1)}, u32[]{:S(2)}, u32[]{:S(2)}) %all-to-all-start.4) | async-done | bytes 65568 | tf_op jit(solution)/shard_map/all_to_all | solution.py:69
  194.0 3.8 %all-to-all-start.3 = ((bf16[32,8,128]{2,1,0:T(8,128)(2,1)}), bf16[32,8,128]{2,1,0:T(8,128)(2,1)S(1)}, u32[]{:S(2)}, u32[]{:S(2)}) async-start(bf16[32,8,128]{2,1,0:T(8,128)(2,1)} %broadcast_in_dim.426), calls=%async_computation.3 | async-start | bytes 131072 | tf_op jit(solution)/shard_map/all_to_all | solution.py:46
  197.9 1.7 fusion.62
  199.6 9.8 %all-to-all-done.3 = bf16[32,8,128]{2,1,0:T(8,128)(2,1)S(1)} async-done(((bf16[32,8,128]{2,1,0:T(8,128)(2,1)}), bf16[32,8,128]{2,1,0:T(8,128)(2,1)S(1)}, u32[]{:S(2)}, u32[]{:S(2)}) %all-to-all-start.3) | async-done | bytes 65568 | tf_op jit(solution)/shard_map/all_to_all | solution.py:46
  210.1 4.6 %all-to-all-start.5 = ((bf16[32,8,128]{2,1,0:T(8,128)(2,1)}), bf16[32,8,128]{2,1,0:T(8,128)(2,1)}, u32[]{:S(2)}, u32[]{:S(2)}) async-start(bf16[32,8,128]{2,1,0:T(8,128)(2,1)} %broadcast_in_dim.447), calls=%async_computation.5 | async-start | bytes 131072 | tf_op jit(solution)/shard_map/all_to_all | solution.py:46
  217.4 8.7 %all-to-all-done.5 = bf16[32,8,128]{2,1,0:T(8,128)(2,1)} async-done(((bf16[32,8,128]{2,1,0:T(8,128)(2,1)}), bf16[32,8,128]{2,1,0:T(8,128)(2,1)}, u32[]{:S(2)}, u32[]{:S(2)}) %all-to-all-start.5) | async-done | bytes 65568 | tf_op jit(solution)/shard_map/all_to_all | solution.py:46
  226.1 1.9 fusion.47
  228.0 20.9 %all-to-all-start.6 = ((bf16[16,16,512]{2,1,0:T(8,128)(2,1)}), bf16[16,16,512]{2,1,0:T(8,128)(2,1)S(1)}, u32[]{:S(2)}, u32[]{:S(2)}) async-start(bf16[16,16,512]{2,1,0:T(8,128)(2,1)} %bitcast.575), calls=%async_computation.6 | async-start | bytes 524288 | tf_op jit(solution)/shard_map/all_to_all | solution.py:69
  249.0 1.5 convolution_bitcast_fusion.9
  250.6 2.5 collective-permute-start.11
  253.1 2.2 collective-permute-start.12
  255.4 3.0 %collective-permute-start.10 = (bf16[1,1,512,128]{3,2,1,0:T(8,128)(2,1)S(1)}, bf16[1,1,512,128]{3,2,1,0:T(8,128)(2,1)S(1)}, u32[]{:S(2)}, u32[]{:S(2)}) collective-permute-start(bf16[1,1,512,128]{3,2,1,0:T(8,128)(2,1)S(1)} %copy-done.45), channel_id=1, source_target_pairs={{0,16},{16,0},{32,48},{48,32},{64,80},{80,64},{96,112},{112,96},{1... | collective-permute-start | bytes 393224 | tf_op jit(solution)/shard_map/ppermute | solution.py:19
  258.4 2.3 collective-permute-start.13
  260.7 3.6 %collective-permute-start.14 = (bf16[1,1,512,128]{3,2,1,0:T(8,128)(2,1)S(1)}, bf16[1,1,512,128]{3,2,1,0:T(8,128)(2,1)S(1)}, u32[]{:S(2)}, u32[]{:S(2)}) collective-permute-start(bf16[1,1,512,128]{3,2,1,0:T(8,128)(2,1)S(1)} %copy-done.43), channel_id=1, source_target_pairs={{0,256},{16,272},{32,288},{48,304},{64,320},{80,336},{96,352},{112... | collective-permute-start | bytes 393224 | tf_op jit(solution)/shard_map/ppermute | solution.py:19
  264.3 2.2 fusion.123
  266.5 1.8 collective-permute-done.11
  268.3 9.2 %collective-permute-done.12 = bf16[1,1,512,128]{3,2,1,0:T(8,128)(2,1)S(1)} collective-permute-done((bf16[1,1,512,128]{3,2,1,0:T(8,128)(2,1)S(1)}, bf16[1,1,512,128]{3,2,1,0:T(8,128)(2,1)S(1)}, u32[]{:S(2)}, u32[]{:S(2)}) %collective-permute-start.12) | collective-permute-done | bytes 131104 | tf_op jit(solution)/shard_map/ppermute | solution.py:19
  (164 shorter events, 28.2 us)
Async XLA Ops:
  0.6 32.8 %copy-start = (bf16[2,512,128]{2,1,0:T(8,128)(2,1)S(1)}, bf16[2,512,128]{2,1,0:T(8,128)(2,1)}, u32[]{:S(2)}) copy-start(bf16[2,512,128]{2,1,0:T(8,128)(2,1)} %param.6) | copy-start | bytes 786436
  0.6 32.8 %copy-start.8 = (bf16[1,512,128]{2,1,0:T(8,128)(2,1)S(1)}, bf16[1,512,128]{2,1,0:T(8,128)(2,1)}, u32[]{:S(2)}) copy-start(bf16[1,512,128]{2,1,0:T(8,128)(2,1)} %param.7) | copy-start | bytes 393220
  0.7 48.6 %collective-permute-start = (bf16[1,1,512,128]{3,2,1,0:T(8,128)(2,1)}, bf16[1,1,512,128]{3,2,1,0:T(8,128)(2,1)S(1)}, u32[]{:S(2)}, u32[]{:S(2)}) collective-permute-start(bf16[1,1,512,128]{3,2,1,0:T(8,128)(2,1)} %bitcast.565), channel_id=1, source_target_pairs={{0,256},{16,272},{32,288},{48,304},{64,320},{80,336},{96,352},{112... | collective-permute-start | bytes 393224 | tf_op jit(solution)/shard_map/ppermute | solution.py:19
  6.3 47.7 %collective-permute-start.1 = (bf16[1,1,512,128]{3,2,1,0:T(8,128)(2,1)}, bf16[1,1,512,128]{3,2,1,0:T(8,128)(2,1)S(1)}, u32[]{:S(2)}, u32[]{:S(2)}) collective-permute-start(bf16[1,1,512,128]{3,2,1,0:T(8,128)(2,1)} %bitcast.566), channel_id=1, source_target_pairs={{0,128},{16,144},{32,160},{48,176},{64,192},{80,208},{96,224},{112... | collective-permute-start | bytes 393224 | tf_op jit(solution)/shard_map/ppermute | solution.py:19
  8.5 47.7 %collective-permute-start.2 = (bf16[1,1,512,128]{3,2,1,0:T(8,128)(2,1)}, bf16[1,1,512,128]{3,2,1,0:T(8,128)(2,1)}, u32[]{:S(2)}, u32[]{:S(2)}) collective-permute-start(bf16[1,1,512,128]{3,2,1,0:T(8,128)(2,1)} %bitcast.567), channel_id=1, source_target_pairs={{0,64},{16,80},{32,96},{48,112},{64,0},{80,16},{96,32},{112,48},{1... | collective-permute-start | bytes 393224 | tf_op jit(solution)/shard_map/ppermute | solution.py:19
  17.3 45.9 %collective-permute-start.3 = (bf16[1,1,512,128]{3,2,1,0:T(8,128)(2,1)}, bf16[1,1,512,128]{3,2,1,0:T(8,128)(2,1)}, u32[]{:S(2)}, u32[]{:S(2)}) collective-permute-start(bf16[1,1,512,128]{3,2,1,0:T(8,128)(2,1)} %bitcast.568), channel_id=1, source_target_pairs={{0,32},{16,48},{32,0},{48,16},{64,96},{80,112},{96,64},{112,80},{1... | collective-permute-start | bytes 393224 | tf_op jit(solution)/shard_map/ppermute | solution.py:19
  22.2 45.0 %collective-permute-start.4 = (bf16[1,1,512,128]{3,2,1,0:T(8,128)(2,1)}, bf16[1,1,512,128]{3,2,1,0:T(8,128)(2,1)}, u32[]{:S(2)}, u32[]{:S(2)}) collective-permute-start(bf16[1,1,512,128]{3,2,1,0:T(8,128)(2,1)} %bitcast.569), channel_id=1, source_target_pairs={{0,16},{16,0},{32,48},{48,32},{64,80},{80,64},{96,112},{112,96},{1... | collective-permute-start | bytes 393224 | tf_op jit(solution)/shard_map/ppermute | solution.py:19
  28.6 5.4 %copy-start.47 = (s32[1,4]{1,0:T(1,128)S(1)}, s32[1,4]{1,0:T(1,128)}, u32[]{:S(2)}) copy-start(s32[1,4]{1,0:T(1,128)} %param.11) | copy-start | bytes 52
  28.6 20.7 %copy-start.21 = (bf16[1,512,128]{2,1,0:T(8,128)(2,1)S(1)}, bf16[1,512,128]{2,1,0:T(8,128)(2,1)}, u32[]{:S(2)}) copy-start(bf16[1,512,128]{2,1,0:T(8,128)(2,1)} %param.8) | copy-start | bytes 393220
  29.6 54.0 %all-to-all-start = ((f32[32,1,2048]{2,1,0:T(1,128)}), f32[32,1,2048]{2,1,0:T(1,128)S(1)}, u32[]{:S(2)}, u32[]{:S(2)}) async-start(f32[32,1,2048]{2,1,0:T(1,128)} %copy.108), calls=%async_computation | async-start | bytes 524288 | tf_op jit(solution)/shard_map/all_to_all | solution.py:29
  49.3 22.2 %collective-permute-start.5 = (bf16[1,1,512,128]{3,2,1,0:T(8,128)(2,1)S(1)}, bf16[1,1,512,128]{3,2,1,0:T(8,128)(2,1)S(1)}, u32[]{:S(2)}, u32[]{:S(2)}) collective-permute-start(bf16[1,1,512,128]{3,2,1,0:T(8,128)(2,1)S(1)} %bitcast.570), channel_id=1, source_target_pairs={{0,256},{16,272},{32,288},{48,304},{64,320},{80,336},{96,352},{112... | collective-permute-start | bytes 393224 | tf_op jit(solution)/shard_map/ppermute | solution.py:19
  53.9 17.6 %collective-permute-start.6 = (bf16[1,1,512,128]{3,2,1,0:T(8,128)(2,1)S(1)}, bf16[1,1,512,128]{3,2,1,0:T(8,128)(2,1)S(1)}, u32[]{:S(2)}, u32[]{:S(2)}) collective-permute-start(bf16[1,1,512,128]{3,2,1,0:T(8,128)(2,1)S(1)} %bitcast.571), channel_id=1, source_target_pairs={{0,128},{16,144},{32,160},{48,176},{64,192},{80,208},{96,224},{112... | collective-permute-start | bytes 393224 | tf_op jit(solution)/shard_map/ppermute | solution.py:19
  56.2 17.5 %collective-permute-start.7 = (bf16[1,1,512,128]{3,2,1,0:T(8,128)(2,1)S(1)}, bf16[1,1,512,128]{3,2,1,0:T(8,128)(2,1)S(1)}, u32[]{:S(2)}, u32[]{:S(2)}) collective-permute-start(bf16[1,1,512,128]{3,2,1,0:T(8,128)(2,1)S(1)} %bitcast.572), channel_id=1, source_target_pairs={{0,64},{16,80},{32,96},{48,112},{64,0},{80,16},{96,32},{112,48},{1... | collective-permute-start | bytes 393224 | tf_op jit(solution)/shard_map/ppermute | solution.py:19
  63.2 12.3 %collective-permute-start.8 = (bf16[1,1,512,128]{3,2,1,0:T(8,128)(2,1)S(1)}, bf16[1,1,512,128]{3,2,1,0:T(8,128)(2,1)S(1)}, u32[]{:S(2)}, u32[]{:S(2)}) collective-permute-start(bf16[1,1,512,128]{3,2,1,0:T(8,128)(2,1)S(1)} %bitcast.573), channel_id=1, source_target_pairs={{0,32},{16,48},{32,0},{48,16},{64,96},{80,112},{96,64},{112,80},{1... | collective-permute-start | bytes 393224 | tf_op jit(solution)/shard_map/ppermute | solution.py:19
  67.3 8.4 %collective-permute-start.9 = (bf16[1,1,512,128]{3,2,1,0:T(8,128)(2,1)S(1)}, bf16[1,1,512,128]{3,2,1,0:T(8,128)(2,1)S(1)}, u32[]{:S(2)}, u32[]{:S(2)}) collective-permute-start(bf16[1,1,512,128]{3,2,1,0:T(8,128)(2,1)S(1)} %bitcast.574), channel_id=1, source_target_pairs={{0,16},{16,0},{32,48},{48,32},{64,80},{80,64},{96,112},{112,96},{1... | collective-permute-start | bytes 393224 | tf_op jit(solution)/shard_map/ppermute | solution.py:19
  71.5 7.9 %copy-start.14 = (bf16[1,1,512,128]{3,2,1,0:T(8,128)(2,1)}, bf16[1,1,512,128]{3,2,1,0:T(8,128)(2,1)S(1)}, u32[]{:S(2)}) copy-start(bf16[1,1,512,128]{3,2,1,0:T(8,128)(2,1)S(1)} %get-tuple-element.39) | copy-start | bytes 393220
  71.5 9.7 %copy-start.17 = (bf16[1,1,512,128]{3,2,1,0:T(8,128)(2,1)}, bf16[1,1,512,128]{3,2,1,0:T(8,128)(2,1)S(1)}, u32[]{:S(2)}) copy-start(bf16[1,1,512,128]{3,2,1,0:T(8,128)(2,1)S(1)} %get-tuple-element.38) | copy-start | bytes 393220
  71.5 5.0 %copy-start.30 = (bf16[1,1,512,128]{3,2,1,0:T(8,128)(2,1)}, bf16[1,1,512,128]{3,2,1,0:T(8,128)(2,1)S(1)}, u32[]{:S(2)}) copy-start(bf16[1,1,512,128]{3,2,1,0:T(8,128)(2,1)S(1)} %collective-permute-done.5) | copy-start | bytes 393220
  71.5 7.8 %copy-start.32 = (bf16[1,1,512,128]{3,2,1,0:T(8,128)(2,1)}, bf16[1,1,512,128]{3,2,1,0:T(8,128)(2,1)S(1)}, u32[]{:S(2)}) copy-start(bf16[1,1,512,128]{3,2,1,0:T(8,128)(2,1)S(1)} %collective-permute-done.6) | copy-start | bytes 393220
  73.7 5.6 %copy-start.34 = (bf16[1,1,512,128]{3,2,1,0:T(8,128)(2,1)}, bf16[1,1,512,128]{3,2,1,0:T(8,128)(2,1)S(1)}, u32[]{:S(2)}) copy-start(bf16[1,1,512,128]{3,2,1,0:T(8,128)(2,1)S(1)} %collective-permute-done.7) | copy-start | bytes 393220
  75.5 3.8 %copy-start.35 = (bf16[1,1,512,128]{3,2,1,0:T(8,128)(2,1)}, bf16[1,1,512,128]{3,2,1,0:T(8,128)(2,1)S(1)}, u32[]{:S(2)}) copy-start(bf16[1,1,512,128]{3,2,1,0:T(8,128)(2,1)S(1)} %collective-permute-done.8) | copy-start | bytes 393220
  75.7 3.7 %copy-start.36 = (bf16[1,1,512,128]{3,2,1,0:T(8,128)(2,1)}, bf16[1,1,512,128]{3,2,1,0:T(8,128)(2,1)S(1)}, u32[]{:S(2)}) copy-start(bf16[1,1,512,128]{3,2,1,0:T(8,128)(2,1)S(1)} %collective-permute-done.9) | copy-start | bytes 393220
  77.5 3.7 %copy-start.15 = (bf16[1,1,512,128]{3,2,1,0:T(8,128)(2,1)}, bf16[1,1,512,128]{3,2,1,0:T(8,128)(2,1)S(1)}, u32[]{:S(2)}) copy-start(bf16[1,1,512,128]{3,2,1,0:T(8,128)(2,1)S(1)} %get-tuple-element.37) | copy-start | bytes 393220
  77.5 22.1 %copy-start.12 = (bf16[1,1,512,128]{3,2,1,0:T(8,128)(2,1)}, bf16[1,1,512,128]{3,2,1,0:T(8,128)(2,1)S(1)}, u32[]{:S(2)}) copy-start(bf16[1,1,512,128]{3,2,1,0:T(8,128)(2,1)S(1)} %get-tuple-element.36) | copy-start | bytes 393220
  81.2 16.6 %copy-start.31 = (bf16[1,1,512,128]{3,2,1,0:T(8,128)(2,1)S(1)}, bf16[1,1,512,128]{3,2,1,0:T(8,128)(2,1)}, u32[]{:S(2)}) copy-start(bf16[1,1,512,128]{3,2,1,0:T(8,128)(2,1)} %copy-done.30) | copy-start | bytes 393220
  81.2 16.7 %copy-start.33 = (bf16[1,1,512,128]{3,2,1,0:T(8,128)(2,1)S(1)}, bf16[1,1,512,128]{3,2,1,0:T(8,128)(2,1)}, u32[]{:S(2)}) copy-start(bf16[1,1,512,128]{3,2,1,0:T(8,128)(2,1)} %copy-done.32) | copy-start | bytes 393220
  86.5 23.0 %all-to-all-start.1 = ((bf16[32,2,1024]{2,1,0:T(2,128)(2,1)}), bf16[32,2,1024]{2,1,0:T(2,128)(2,1)S(1)}, u32[]{:S(2)}, u32[]{:S(2)}) async-start(bf16[32,2,1024]{2,1,0:T(2,128)(2,1)} %reshape.682), calls=%async_computation.1 | async-start | bytes 262144 | tf_op jit(solution)/shard_map/all_to_all | solution.py:46
  112.2 3.8 %copy-start.2 = (f32[512,2,512]{2,0,1:T(8,128)S(1)}, f32[512,2,512]{2,0,1:T(8,128)}, u32[]{:S(2)}) copy-start(f32[512,2,512]{2,0,1:T(8,128)} %get-tuple-element.61) | copy-start | bytes 6291460
  116.0 4.2 %copy-start.4 = (f32[512,2,512]{2,0,1:T(8,128)S(1)}, f32[512,2,512]{2,0,1:T(8,128)}, u32[]{:S(2)}) copy-start(f32[512,2,512]{2,0,1:T(8,128)} %get-tuple-element.67) | copy-start | bytes 6291460
  116.0 4.2 %copy-start.41 = (bf16[2,512,128]{2,1,0:T(8,128)(2,1)S(1)}, bf16[2,512,128]{2,1,0:T(8,128)(2,1)}, u32[]{:S(2)}) copy-start(bf16[2,512,128]{2,1,0:T(8,128)(2,1)} %param.9) | copy-start | bytes 786436
  134.5 3.8 %copy-start.18 = (bf16[1,1,512,128]{3,2,1,0:T(8,128)(2,1)S(1)}, bf16[1,1,512,128]{3,2,1,0:T(8,128)(2,1)}, u32[]{:S(2)}) copy-start(bf16[1,1,512,128]{3,2,1,0:T(8,128)(2,1)} %copy-done.17) | copy-start | bytes 393220
  135.7 4.0 %copy-start.46 = (bf16[256,128,1]{1,0,2:T(8,128)(2,1)S(1)}, bf16[256,128,1]{1,0,2:T(8,128)(2,1)}, u32[]{:S(2)}) copy-start(bf16[256,128,1]{1,0,2:T(8,128)(2,1)} %reshape.664) | copy-start | bytes 196612
  142.1 35.8 %all-to-all-start.2 = ((bf16[32,8,128]{2,1,0:T(8,128)(2,1)}), bf16[32,8,128]{2,1,0:T(8,128)(2,1)}, u32[]{:S(2)}, u32[]{:S(2)}) async-start(bf16[32,8,128]{2,1,0:T(8,128)(2,1)} %fusion.70), calls=%async_computation.2 | async-start | bytes 131072 | tf_op jit(solution)/shard_map/all_to_all | solution.py:69
  149.0 26.1 %copy-start.5 = (bf16[2,512,512]{1,2,0:T(8,128)(2,1)S(1)}, bf16[2,512,512]{1,2,0:T(8,128)(2,1)}, u32[]{:S(2)}) copy-start(bf16[2,512,512]{1,2,0:T(8,128)(2,1)} %fusion.14) | copy-start | bytes 3145732
  149.0 26.1 %copy-start.16 = (bf16[1,1,512,128]{3,2,1,0:T(8,128)(2,1)S(1)}, bf16[1,1,512,128]{3,2,1,0:T(8,128)(2,1)}, u32[]{:S(2)}) copy-start(bf16[1,1,512,128]{3,2,1,0:T(8,128)(2,1)} %copy-done.15) | copy-start | bytes 393220
  149.0 101.6 %collective-permute-start.16 = (bf16[1,1,512,128]{3,2,1,0:T(8,128)(2,1)}, bf16[1,1,512,128]{3,2,1,0:T(8,128)(2,1)}, u32[]{:S(2)}, u32[]{:S(2)}) collective-permute-start(bf16[1,1,512,128]{3,2,1,0:T(8,128)(2,1)} %get-tuple-element.43), channel_id=1, source_target_pairs={{0,32},{16,48},{32,0},{48,16},{64,96},{80,112},{96,64},{112,80},{1... | collective-permute-start | bytes 393224 | tf_op jit(solution)/shard_map/ppermute | solution.py:19
  153.1 100.0 %collective-permute-start.17 = (bf16[1,1,512,128]{3,2,1,0:T(8,128)(2,1)}, bf16[1,1,512,128]{3,2,1,0:T(8,128)(2,1)}, u32[]{:S(2)}, u32[]{:S(2)}) collective-permute-start(bf16[1,1,512,128]{3,2,1,0:T(8,128)(2,1)} %get-tuple-element.44), channel_id=1, source_target_pairs={{0,64},{16,80},{32,96},{48,112},{64,0},{80,16},{96,32},{112,48},{1... | collective-permute-start | bytes 393224 | tf_op jit(solution)/shard_map/ppermute | solution.py:19
  160.1 95.3 %collective-permute-start.15 = (bf16[1,1,512,128]{3,2,1,0:T(8,128)(2,1)}, bf16[1,1,512,128]{3,2,1,0:T(8,128)(2,1)}, u32[]{:S(2)}, u32[]{:S(2)}) collective-permute-start(bf16[1,1,512,128]{3,2,1,0:T(8,128)(2,1)} %get-tuple-element.40), channel_id=1, source_target_pairs={{0,16},{16,0},{32,48},{48,32},{64,80},{80,64},{96,112},{112,96},{1... | collective-permute-start | bytes 393224 | tf_op jit(solution)/shard_map/ppermute | solution.py:19
  163.2 95.2 %collective-permute-start.18 = (bf16[1,1,512,128]{3,2,1,0:T(8,128)(2,1)}, bf16[1,1,512,128]{3,2,1,0:T(8,128)(2,1)}, u32[]{:S(2)}, u32[]{:S(2)}) collective-permute-start(bf16[1,1,512,128]{3,2,1,0:T(8,128)(2,1)} %get-tuple-element.42), channel_id=1, source_target_pairs={{0,128},{16,144},{32,160},{48,176},{64,192},{80,208},{96,224},{112... | collective-permute-start | bytes 393224 | tf_op jit(solution)/shard_map/ppermute | solution.py:19
  166.3 9.3 %copy-start.6 = (bf16[2,512,512]{1,2,0:T(8,128)(2,1)S(1)}, bf16[2,512,512]{1,2,0:T(8,128)(2,1)}, u32[]{:S(2)}) copy-start(bf16[2,512,512]{1,2,0:T(8,128)(2,1)} %fusion.11) | copy-start | bytes 3145732
  166.3 9.3 %copy-start.9 = (f32[128,2,512]{0,2,1:T(8,128)S(1)}, f32[128,2,512]{0,2,1:T(8,128)}, u32[]{:S(2)}) copy-start(f32[128,2,512]{0,2,1:T(8,128)} %convolution_bitcast_fusion.1) | copy-start | bytes 1572868
  166.3 9.3 %copy-start.10 = (f32[128,2,512]{0,2,1:T(8,128)S(1)}, f32[128,2,512]{0,2,1:T(8,128)}, u32[]{:S(2)}) copy-start(f32[128,2,512]{0,2,1:T(8,128)} %fusion.142) | copy-start | bytes 1572868
  166.3 9.3 %copy-start.11 = (f32[1,2,1,512,128]{4,3,1,2,0:T(8,128)S(1)}, f32[1,2,1,512,128]{4,3,1,2,0:T(8,128)}, u32[]{:S(2)}) copy-start(f32[1,2,1,512,128]{4,3,1,2,0:T(8,128)} %convolution_bitcast_fusion) | copy-start | bytes 1572868
  166.3 9.3 %copy-start.13 = (bf16[1,1,512,128]{3,2,1,0:T(8,128)(2,1)S(1)}, bf16[1,1,512,128]{3,2,1,0:T(8,128)(2,1)}, u32[]{:S(2)}) copy-start(bf16[1,1,512,128]{3,2,1,0:T(8,128)(2,1)} %copy-done.12) | copy-start | bytes 393220
  166.3 94.4 %collective-permute-start.19 = (bf16[1,1,512,128]{3,2,1,0:T(8,128)(2,1)}, bf16[1,1,512,128]{3,2,1,0:T(8,128)(2,1)}, u32[]{:S(2)}, u32[]{:S(2)}) collective-permute-start(bf16[1,1,512,128]{3,2,1,0:T(8,128)(2,1)} %get-tuple-element.41), channel_id=1, source_target_pairs={{0,256},{16,272},{32,288},{48,304},{64,320},{80,336},{96,352},{112... | collective-permute-start | bytes 393224 | tf_op jit(solution)/shard_map/ppermute | solution.py:19
  177.9 36.7 %copy-start.19 = (bf16[512,128]{1,0:T(8,128)(2,1)S(1)}, bf16[512,128]{1,0:T(8,128)(2,1)}, u32[]{:S(2)}) copy-start(bf16[512,128]{1,0:T(8,128)(2,1)} %fusion.64) | copy-start | bytes 393220
  177.9 36.7 %copy-start.20 = (bf16[512,128]{1,0:T(8,128)(2,1)S(1)}, bf16[512,128]{1,0:T(8,128)(2,1)}, u32[]{:S(2)}) copy-start(bf16[512,128]{1,0:T(8,128)(2,1)} %fusion.65) | copy-start | bytes 393220
  177.9 15.5 %all-to-all-start.4 = ((bf16[32,8,128]{2,1,0:T(8,128)(2,1)}), bf16[32,8,128]{2,1,0:T(8,128)(2,1)S(1)}, u32[]{:S(2)}, u32[]{:S(2)}) async-start(bf16[32,8,128]{2,1,0:T(8,128)(2,1)} %fusion.69), calls=%async_computation.4 | async-start | bytes 131072 | tf_op jit(solution)/shard_map/all_to_all | solution.py:69
  181.9 33.5 %copy-start.24 = (bf16[2,512,128]{1,2,0:T(8,128)(2,1)S(1)}, bf16[2,512,128]{1,2,0:T(8,128)(2,1)}, u32[]{:S(2)}) copy-start(bf16[2,512,128]{1,2,0:T(8,128)(2,1)} %get-tuple-element.51) | copy-start | bytes 786436
  194.0 15.3 %all-to-all-start.3 = ((bf16[32,8,128]{2,1,0:T(8,128)(2,1)}), bf16[32,8,128]{2,1,0:T(8,128)(2,1)S(1)}, u32[]{:S(2)}, u32[]{:S(2)}) async-start(bf16[32,8,128]{2,1,0:T(8,128)(2,1)} %broadcast_in_dim.426), calls=%async_computation.3 | async-start | bytes 131072 | tf_op jit(solution)/shard_map/all_to_all | solution.py:46
  209.4 6.1 %copy-start.27 = (bf16[32,8,128]{2,1,0:T(8,128)(2,1)}, bf16[32,8,128]{2,1,0:T(8,128)(2,1)S(1)}, u32[]{:S(2)}) copy-start(bf16[32,8,128]{2,1,0:T(8,128)(2,1)S(1)} %all-to-all-done.3) | copy-start | bytes 196612
  210.1 16.1 %all-to-all-start.5 = ((bf16[32,8,128]{2,1,0:T(8,128)(2,1)}), bf16[32,8,128]{2,1,0:T(8,128)(2,1)}, u32[]{:S(2)}, u32[]{:S(2)}) async-start(bf16[32,8,128]{2,1,0:T(8,128)(2,1)} %broadcast_in_dim.447), calls=%async_computation.5 | async-start | bytes 131072 | tf_op jit(solution)/shard_map/all_to_all | solution.py:46
  228.0 50.6 %all-to-all-start.6 = ((bf16[16,16,512]{2,1,0:T(8,128)(2,1)}), bf16[16,16,512]{2,1,0:T(8,128)(2,1)S(1)}, u32[]{:S(2)}, u32[]{:S(2)}) async-start(bf16[16,16,512]{2,1,0:T(8,128)(2,1)} %bitcast.575), calls=%async_computation.6 | async-start | bytes 524288 | tf_op jit(solution)/shard_map/all_to_all | solution.py:69
  248.9 6.4 %copy-start.45 = (bf16[1,1,512,128]{3,2,1,0:T(8,128)(2,1)S(1)}, bf16[1,1,512,128]{3,2,1,0:T(8,128)(2,1)}, u32[]{:S(2)}) copy-start(bf16[1,1,512,128]{3,2,1,0:T(8,128)(2,1)} %get-tuple-element.45) | copy-start | bytes 393220
  248.9 9.5 %copy-start.44 = (bf16[1,1,512,128]{3,2,1,0:T(8,128)(2,1)S(1)}, bf16[1,1,512,128]{3,2,1,0:T(8,128)(2,1)}, u32[]{:S(2)}) copy-start(bf16[1,1,512,128]{3,2,1,0:T(8,128)(2,1)} %get-tuple-element.47) | copy-start | bytes 393220
  248.9 11.8 %copy-start.43 = (bf16[1,1,512,128]{3,2,1,0:T(8,128)(2,1)S(1)}, bf16[1,1,512,128]{3,2,1,0:T(8,128)(2,1)}, u32[]{:S(2)}) copy-start(bf16[1,1,512,128]{3,2,1,0:T(8,128)(2,1)} %get-tuple-element.46) | copy-start | bytes 393220
  249.0 15.4 %copy-start.7 = (bf16[256,512]{1,0:T(8,128)(2,1)S(1)}, bf16[256,512]{1,0:T(8,128)(2,1)}, u32[]{:S(2)}) copy-start(bf16[256,512]{1,0:T(8,128)(2,1)} %param.10) | copy-start | bytes 786436
  250.5 27.1 %copy-start.25 = (f32[512,128]{1,0:T(8,128)S(1)}, f32[512,128]{1,0:T(8,128)}, u32[]{:S(2)}) copy-start(f32[512,128]{1,0:T(8,128)} %fusion.56) | copy-start | bytes 786436
  250.5 27.1 %copy-start.28 = (bf16[32,8,128]{2,1,0:T(8,128)(2,1)S(1)}, bf16[32,8,128]{2,1,0:T(8,128)(2,1)}, u32[]{:S(2)}) copy-start(bf16[32,8,128]{2,1,0:T(8,128)(2,1)} %copy-done.27) | copy-start | bytes 196612
  250.6 17.7 %collective-permute-start.11 = (bf16[1,1,512,128]{3,2,1,0:T(8,128)(2,1)S(1)}, bf16[1,1,512,128]{3,2,1,0:T(8,128)(2,1)S(1)}, u32[]{:S(2)}, u32[]{:S(2)}) collective-permute-start(bf16[1,1,512,128]{3,2,1,0:T(8,128)(2,1)S(1)} %get-tuple-element.48), channel_id=1, source_target_pairs={{0,32},{16,48},{32,0},{48,16},{64,96},{80,112},{96,64},{112,80},{1... | collective-permute-start | bytes 393224 | tf_op jit(solution)/shard_map/ppermute | solution.py:19
  253.1 24.4 %collective-permute-start.12 = (bf16[1,1,512,128]{3,2,1,0:T(8,128)(2,1)S(1)}, bf16[1,1,512,128]{3,2,1,0:T(8,128)(2,1)S(1)}, u32[]{:S(2)}, u32[]{:S(2)}) collective-permute-start(bf16[1,1,512,128]{3,2,1,0:T(8,128)(2,1)S(1)} %get-tuple-element.49), channel_id=1, source_target_pairs={{0,64},{16,80},{32,96},{48,112},{64,0},{80,16},{96,32},{112,48},{1... | collective-permute-start | bytes 393224 | tf_op jit(solution)/shard_map/ppermute | solution.py:19
  255.4 22.2 %collective-permute-start.10 = (bf16[1,1,512,128]{3,2,1,0:T(8,128)(2,1)S(1)}, bf16[1,1,512,128]{3,2,1,0:T(8,128)(2,1)S(1)}, u32[]{:S(2)}, u32[]{:S(2)}) collective-permute-start(bf16[1,1,512,128]{3,2,1,0:T(8,128)(2,1)S(1)} %copy-done.45), channel_id=1, source_target_pairs={{0,16},{16,0},{32,48},{48,32},{64,80},{80,64},{96,112},{112,96},{1... | collective-permute-start | bytes 393224 | tf_op jit(solution)/shard_map/ppermute | solution.py:19
  258.4 19.1 %collective-permute-start.13 = (bf16[1,1,512,128]{3,2,1,0:T(8,128)(2,1)S(1)}, bf16[1,1,512,128]{3,2,1,0:T(8,128)(2,1)S(1)}, u32[]{:S(2)}, u32[]{:S(2)}) collective-permute-start(bf16[1,1,512,128]{3,2,1,0:T(8,128)(2,1)S(1)} %copy-done.44), channel_id=1, source_target_pairs={{0,128},{16,144},{32,160},{48,176},{64,192},{80,208},{96,224},{112... | collective-permute-start | bytes 393224 | tf_op jit(solution)/shard_map/ppermute | solution.py:19
  260.7 16.8 %collective-permute-start.14 = (bf16[1,1,512,128]{3,2,1,0:T(8,128)(2,1)S(1)}, bf16[1,1,512,128]{3,2,1,0:T(8,128)(2,1)S(1)}, u32[]{:S(2)}, u32[]{:S(2)}) collective-permute-start(bf16[1,1,512,128]{3,2,1,0:T(8,128)(2,1)S(1)} %copy-done.43), channel_id=1, source_target_pairs={{0,256},{16,272},{32,288},{48,304},{64,320},{80,336},{96,352},{112... | collective-permute-start | bytes 393224 | tf_op jit(solution)/shard_map/ppermute | solution.py:19
  (11 other events, 16.7 us)
where the time goes:
time: 281 us; the launch traced here: 279 us
  starting transfers between devices  137 us (49%)
  matrix products  51 us (18%)
  waiting for transfers between devices  50.2 us (18%)
  other arithmetic  15.4 us (5%)
  between operations  14.7 us (5%)
  local copies, waits for them, and re-layouts  11.1 us (4%)
    ppermute x20, starting transfers between devices, from_partner(): return lax.ppermute(value, axis, pairs)  81.5 us
    all_to_all x3, starting transfers between devices, sent_and_summed(): lax.all_to_all(tiles, axis, split_axis=0, concat_axis=0, tiled=True)  31.8 us
    all_to_all x3, waiting for transfers between devices, copy_for_each(): return lax.all_to_all(copies, axis, split_axis=0, concat_axis=0, tiled=True)  26 us
    all_to_all x3, starting transfers between devices, copy_for_each(): return lax.all_to_all(copies, axis, split_axis=0, concat_axis=0, tiled=True)  19.7 us
    ppermute x20, waiting for transfers between devices, from_partner(): return lax.ppermute(value, axis, pairs)  15.3 us
    dot_general x10, matrix products, pair_products(): jnp.einsum('hgbqd,hbkd->hgbqk', left_side, right_side, preferred_element_...  15 us
    dot_general x10, matrix products, back_rows(): jnp.einsum('hgbqk,hgbqd->hbkd', weights, left_side, preferred_element_typ...  11.6 us
    dot_general x10, matrix products, mix_rows(): jnp.einsum('hgbqk,hbkd->hgbqd', weights, right_side, preferred_element_ty...  10.9 us
  transfers between devices with their start and end apart: 27, of which 9 were waited for; matrix products, arithmetic and copies ran while one was open for 15% of the time, Pallas kernels for 0%

commit v1 on v0

v1 whole, which is shorter than its diff:
```python
import functools
import math

import jax
import jax.numpy as jnp
from jax import lax
from jax.experimental import pallas as pl
from jax.experimental.pallas import tpu as pltpu
from jax.sharding import PartitionSpec as P

MESH = pl.DeviceIdType.MESH
BLOCK = 512
DIM = 128
ROWS = 1024
SUM = 256
CHUNK = 512
SCALE = 1.0 / 12.0
EXP2_SCALE = math.log2(math.e) / 12.0
F32, BF16 = jnp.float32, jnp.bfloat16

ORDER = (3, 0, 4, 1, 2)
Z_MASKS = tuple(range(1, 8))
X_MASKS = (8, 16, 24)
Y_MASKS = (4, 8, 12)

OWN, SLOT, SUMMARY = 0, 1, 5


def flipped(index, mask):
    out = index
    bit = 1
    while bit <= mask:
        if mask & bit:
            out = out + bit * (1 - 2 * lax.rem(lax.div(index, bit), 2))
        bit *= 2
    return out


def dot(a, b):
    return lax.dot_general(a, b, (((1,), (0,)), ((), ())), preferred_element_type=F32)


def dot_nt(a, b):
    return lax.dot_general(a, b, (((1,), (1,)), ((), ())), preferred_element_type=F32)


def dot_tn(a, b):
    return lax.dot_general(a, b, (((0,), (0,)), ((), ())), preferred_element_type=F32)


def kernel(
    bits_ref, q_ref, k_ref, v_ref, do_ref, proj_ref,
    out_ref, dq_ref, dk_ref, dv_ref, dproj_ref,
    qt, dot_t, part, rx, s8, rz, agz, agx,
    kr, vr, ks, vs, e_ref, m_ref, l_ref, mslot, acc, dqt,
    gka, gva, own_gk, own_gv, gslot_k, gslot_v, gk, gv, rgk, rgv,
    part2, rx2, s82, rz2, agz2, agx2,
    t_ref, rc, u_ref, ry, w_ref, rh,
    send_sem, recv_sem,
):
    seq = lax.axis_index("seq")
    head = lax.axis_index("head")
    my_x, my_z = lax.div(seq, 8), lax.rem(seq, 8)
    my_y, my_hi, my_core = lax.div(head, 4), lax.rem(lax.div(head, 2), 2), lax.rem(head, 2)

    barrier = pltpu.get_barrier_semaphore()
    peers = [("seq", m) for m in Z_MASKS + X_MASKS] + [("head", m) for m in (1, 2) + Y_MASKS]
    for axis, mask in peers:
        me = seq if axis == "seq" else head
        pl.semaphore_signal(barrier, inc=1, device_id={axis: flipped(me, mask)}, device_id_type=MESH)

    ids = iter(range(200))

    def copy(src, dst, axis, mask):
        me = seq if axis == "seq" else head
        n = next(ids)
        c = pltpu.make_async_remote_copy(
            src_ref=src, dst_ref=dst, send_sem=send_sem.at[n], recv_sem=recv_sem.at[n],
            device_id={axis: flipped(me, mask)}, device_id_type=MESH,
        )
        c.start()
        sent.append(c)
        return c

    sent = []

    proj = proj_ref[...]
    part[0:16] = dot(proj, k_ref[...]).reshape(16, 16, DIM)
    part[16:32] = dot(proj, v_ref[...]).reshape(16, 16, DIM)
    qt[...] = q_ref[...].T
    dot_t[...] = do_ref[...].T

    missing = 10 - (bits_ref[0, 0] + bits_ref[0, 1] + bits_ref[0, 2] + bits_ref[0, 3])
    place = jnp.int32(0)
    for i, b in enumerate(ORDER):
        place = place + jnp.where(missing == b, i, 0)

    pl.semaphore_wait(barrier, len(peers))

    def fetch(i):
        mask = 1 << ORDER[i]
        return (
            copy(k_ref, kr.at[i], "seq", mask),
            copy(v_ref, vr.at[i], "seq", mask),
        )

    def wait_recv(cs):
        for c in cs:
            c.wait_recv()

    def scatter_x(src, dst):
        return [
            copy(src.at[pl.ds(lax.div(flipped(seq, m), 8) * 8, 8)], dst.at[j], "seq", m)
            for j, m in enumerate(X_MASKS)
        ]

    def scatter_z(src, dst):
        return [
            copy(src.at[lax.rem(flipped(seq, m), 8)], dst.at[j], "seq", m)
            for j, m in enumerate(Z_MASKS)
        ]

    def gather_z(buf):
        return [copy(buf.at[my_z], buf.at[my_z], "seq", m) for m in Z_MASKS]

    def gather_x(src, dst):
        return [copy(src, dst.at[my_x], "seq", m) for m in X_MASKS]

    def forward(row, n, k, v, first=False):
        base = row * BLOCK

        def step(c, carry):
            cols = pl.ds(pl.multiple_of(c * CHUNK, CHUNK), CHUNK)
            s = dot(k[...], qt[:, cols])
            top = jnp.max(s, axis=0, keepdims=True)
            if not first:
                before = m_ref[:, cols]
                top = jnp.maximum(before, top)
                alpha = jnp.exp2((before - top) * EXP2_SCALE)
            e = jnp.exp2((s - top) * EXP2_SCALE)
            total = jnp.sum(e, axis=0, keepdims=True)
            eb = e.astype(BF16)
            e_ref[base : base + n, cols] = eb
            mixed = dot_tn(v[...], eb)
            if not first:
                total = l_ref[:, cols] * alpha + total
                mixed = acc[:, cols] * alpha + mixed
            l_ref[:, cols] = total
            acc[:, cols] = mixed
            m_ref[:, cols] = top
            mslot[row : row + 1, cols] = top
            return carry

        lax.fori_loop(0, ROWS // CHUNK, step, 0)

    def choose(i):
        early = i < place
        ks[i] = jnp.where(early, kr[i], kr[i + 1])
        vs[i] = jnp.where(early, vr[i], vr[i + 1])

    xs = scatter_x(part, rx)
    f_x1 = fetch(0)
    f_z1 = fetch(1)
    f_x2 = fetch(2)
    forward(OWN, BLOCK, k_ref, v_ref, first=True)
    wait_recv(xs)
    mine = part[pl.ds(my_x * 8, 8)]
    s8[...] = mine + rx[0] + rx[1] + rx[2]
    zs = scatter_z(s8, rz)
    f_z2 = fetch(3)
    wait_recv(f_x1 + f_z1)
    choose(0)
    forward(SLOT, BLOCK, ks.at[0], vs.at[0])
    wait_recv(zs)
    total = s8[my_z]
    for j in range(7):
        total = total + rz[j]
    agz[my_z] = total.astype(BF16)
    zg = gather_z(agz)
    f_z4 = fetch(4)
    wait_recv(f_x2)
    choose(1)
    forward(SLOT + 1, BLOCK, ks.at[1], vs.at[1])
    wait_recv(zg)
    xg = gather_x(agz, agx)
    agx[my_x] = agz[...]
    wait_recv(f_z2)
    choose(2)
    forward(SLOT + 2, BLOCK, ks.at[2], vs.at[2])
    wait_recv(xg)
    summary_k = agx[0:2].reshape(SUM, DIM)
    summary_v = agx[2:4].reshape(SUM, DIM)
    sk, sv = ks.at[4, 0:SUM], vs.at[4, 0:SUM]
    sk[...] = summary_k
    sv[...] = summary_v
    forward(SUMMARY, SUM, sk, sv)
    wait_recv(f_z4)
    choose(3)
    forward(SLOT + 3, BLOCK, ks.at[3], vs.at[3])

    inverse = 1.0 / l_ref[...]
    attended = acc[...] * inverse
    delta = jnp.sum(attended * dot_t[...].astype(F32), axis=0, keepdims=True)
    l_ref[...] = inverse
    acc[0:1, :] = delta
    out_ref[...] = attended.T.astype(BF16)
    dqt[...] = jnp.zeros_like(dqt)

    def backward(row, n, k, v, gk_acc, gv_acc):
        base = row * BLOCK
        gk_acc[...] = jnp.zeros_like(gk_acc)
        gv_acc[...] = jnp.zeros_like(gv_acc)

        def step(c, carry):
            cols = pl.ds(pl.multiple_of(c * CHUNK, CHUNK), CHUNK)
            factor = jnp.exp2((mslot[row : row + 1, cols] - m_ref[:, cols]) * EXP2_SCALE) * l_ref[:, cols]
            p = e_ref[base : base + n, cols].astype(F32) * factor
            dp = dot(v[...], dot_t[:, cols])
            ds = (p * (dp - acc[0:1, cols])).astype(BF16)
            dqt[:, cols] += dot_tn(k[...], ds)
            gk_acc[...] += dot(ds, q_ref[cols, :])
            gv_acc[...] += dot(p.astype(BF16), do_ref[cols, :])
            return carry

        lax.fori_loop(0, ROWS // CHUNK, step, 0)

    half_k, half_v = gka.at[0:SUM], gva.at[0:SUM]
    backward(SUMMARY, SUM, sk, sv, half_k, half_v)
    part2[0:16] = (half_k[...] * SCALE).astype(BF16).reshape(16, 16, DIM)
    part2[16:32] = half_v[...].astype(BF16).reshape(16, 16, DIM)
    xs = scatter_x(part2, rx2)

    def slot_back(i):
        backward(SLOT + i, BLOCK, ks.at[i], vs.at[i], gka, gva)
        gslot_k[i] = (gka[...] * SCALE).astype(BF16)
        gslot_v[i] = gva[...].astype(BF16)

    def give_back(i):
        for slots, g in ((gslot_k, gk), (gslot_v, gv)):
            zero = jnp.zeros((BLOCK, DIM), BF16)
            early = slots[i] if i < 4 else zero
            late = slots[i - 1] if i > 0 else zero
            g[i] = jnp.where(i < place, early, jnp.where(i > place, late, zero))
        mask = 1 << ORDER[i]
        return (
            copy(gk.at[i], rgk.at[i], "seq", mask),
            copy(gv.at[i], rgv.at[i], "seq", mask),
        )

    slot_back(3)
    wait_recv(xs)
    s82[...] = (
        part2[pl.ds(my_x * 8, 8)].astype(F32) + rx2[0].astype(F32) + rx2[1].astype(F32) + rx2[2].astype(F32)
    )
    zs = scatter_z(s82, rz2)
    slot_back(2)
    r_z2 = give_back(3)
    slot_back(1)
    wait_recv(zs)
    total = s82[my_z]
    for j in range(7):
        total = total + rz2[j]
    agz2[my_z] = total.astype(BF16)
    zg = gather_z(agz2)
    r_z4 = give_back(4)
    r_x2 = give_back(2)
    slot_back(0)
    r_z1 = give_back(1)
    r_x1 = give_back(0)
    wait_recv(zg)
    xg = gather_x(agz2, agx2)
    agx2[my_x] = agz2[...]
    backward(OWN, BLOCK, k_ref, v_ref, own_gk, own_gv)
    dq_ref[...] = (dqt[...] * SCALE).T.astype(BF16)
    wait_recv(xg)
    sg_k = agx2[0:2].reshape(SUM, DIM)
    sg_v = agx2[2:4].reshape(SUM, DIM)
    term = dot_nt(sg_k, k_ref[...]) + dot_nt(sg_v, v_ref[...])
    term = term.astype(BF16).reshape(8, 2, 16, BLOCK)
    t_ref[0] = term[:, 0]
    t_ref[1] = term[:, 1]
    c_core = copy(t_ref.at[1 - my_core], rc, "head", 1)
    own_gk[...] = own_gk[...] * SCALE + dot_tn(proj_ref[...], sg_k)
    own_gv[...] = own_gv[...] + dot_tn(proj_ref[...], sg_v)
    c_core.wait_recv()
    u_ref[...] = (t_ref[my_core].astype(F32) + rc[...].astype(F32)).astype(BF16).reshape(4, 2, 16, BLOCK)
    ys = [
        copy(u_ref.at[lax.div(flipped(head, m), 4)], ry.at[j], "head", m)
        for j, m in enumerate(Y_MASKS)
    ]
    wait_recv(ys)
    w_ref[...] = u_ref[my_y].astype(F32) + ry[0].astype(F32) + ry[1].astype(F32) + ry[2].astype(F32)
    hs = copy(w_ref.at[1 - my_hi], rh, "head", 2)
    for c, i in ((r_x1, 0), (r_x2, 2), (r_z1, 1), (r_z2, 3)):
        wait_recv(c)
        own_gk[...] += rgk[i].astype(F32)
        own_gv[...] += rgv[i].astype(F32)
    wait_recv(r_z4)
    dk_ref[...] = (own_gk[...] + rgk[4].astype(F32)).astype(BF16)
    dv_ref[...] = (own_gv[...] + rgv[4].astype(F32)).astype(BF16)
    hs.wait_recv()
    dproj_ref[...] = w_ref[my_hi] + rh[...]
    for c in sent:
        c.wait_send()


def per_device(queries, key_tokens, value_tokens, output_gradient, summary_proj, partner_bits):
    vmem = pl.BlockSpec(memory_space=pltpu.VMEM)
    smem = pl.BlockSpec(memory_space=pltpu.SMEM)
    V = pltpu.VMEM
    copies = 68
    out, dq, dk, dv, dproj = pl.pallas_call(
        kernel,
        name="butterfly",
        out_shape=(
            jax.ShapeDtypeStruct((ROWS, DIM), BF16),
            jax.ShapeDtypeStruct((ROWS, DIM), BF16),
            jax.ShapeDtypeStruct((BLOCK, DIM), BF16),
            jax.ShapeDtypeStruct((BLOCK, DIM), BF16),
            jax.ShapeDtypeStruct((16, BLOCK), F32),
        ),
        in_specs=[smem] + [vmem] * 5,
        out_specs=[vmem] * 5,
        scratch_shapes=[
            V((DIM, ROWS), BF16), V((DIM, ROWS), BF16),
            V((32, 16, DIM), F32), V((3, 8, 16, DIM), F32),
            V((8, 16, DIM), F32), V((7, 16, DIM), F32),
            V((8, 16, DIM), BF16), V((4, 8, 16, DIM), BF16),
            V((5, BLOCK, DIM), BF16), V((5, BLOCK, DIM), BF16),
            V((5, BLOCK, DIM), BF16), V((5, BLOCK, DIM), BF16),
            V((5 * BLOCK + SUM, ROWS), BF16),
            V((1, ROWS), F32), V((1, ROWS), F32), V((8, ROWS), F32),
            V((DIM, ROWS), F32), V((DIM, ROWS), F32),
            V((BLOCK, DIM), F32), V((BLOCK, DIM), F32),
            V((BLOCK, DIM), F32), V((BLOCK, DIM), F32),
            V((4, BLOCK, DIM), BF16), V((4, BLOCK, DIM), BF16),
            V((5, BLOCK, DIM), BF16), V((5, BLOCK, DIM), BF16),
            V((5, BLOCK, DIM), BF16), V((5, BLOCK, DIM), BF16),
            V((32, 16, DIM), BF16), V((3, 8, 16, DIM), BF16),
            V((8, 16, DIM), F32), V((7, 16, DIM), F32),
            V((8, 16, DIM), BF16), V((4, 8, 16, DIM), BF16),
            V((2, 8, 16, BLOCK), BF16), V((8, 16, BLOCK), BF16),
            V((4, 2, 16, BLOCK), BF16), V((3, 2, 16, BLOCK), BF16),
            V((2, 16, BLOCK), F32), V((16, BLOCK), F32),
            pltpu.SemaphoreType.DMA((copies,)), pltpu.SemaphoreType.DMA((copies,)),
        ],
        compiler_params=pltpu.CompilerParams(
            collective_id=0, has_side_effects=True, vmem_limit_bytes=60 * 1024 * 1024
        ),
    )(
        partner_bits,
        queries.reshape(ROWS, DIM),
        key_tokens.reshape(BLOCK, DIM),
        value_tokens.reshape(BLOCK, DIM),
        output_gradient.reshape(ROWS, DIM),
        summary_proj,
    )
    return (
        out.reshape(queries.shape),
        dq.reshape(queries.shape),
        dk.reshape(key_tokens.shape),
        dv.reshape(value_tokens.shape),
        dproj,
    )


def solution(mesh):
    rows = P("head", "seq", None)
    return jax.shard_map(
        per_device,
        mesh=mesh,
        in_specs=(rows, rows, rows, rows, P(None, "seq"), P("seq", None)),
        out_specs=(rows, rows, rows, rows, P("head", "seq")),
        check_vma=False,
    )
```

time: 281 us -> 114 us (0.41)
  starting transfers between devices: 137 us -> 0 us
  Pallas kernels: 0 us -> 108 us
  matrix products: 51 us -> 0 us
  waiting for transfers between devices: 50.2 us -> 0 us
  other arithmetic: 15.4 us -> 0 us
  between operations: 14.7 us -> 0.66 us
  local copies, waits for them, and re-layouts: 11.1 us -> 5.04 us
    pallas_call x0 -> x1, Pallas kernels: none -> 108 us  [per_device(): pl.pallas_call(kernel, name='butterfly', out_shape=(jax.ShapeDtypeStruct(...]
    ppermute x20 -> x0, starting transfers between devices: 81.5 us -> none  [from_partner(): return lax.ppermute(value, axis, pairs)]
    all_to_all x7 -> x0, starting transfers between devices: 55.3 us -> none  [the longest x3 31.8 us: sent_and_summed(): lax.all_to_all(tiles, axis, split_axis=0, concat_axis=0, tiled=True)]
    dot_general x42 -> x0, matrix products: 51 us -> none  [the longest x10 15 us: pair_products(): jnp.einsum('hgbqd,hbkd->hgbqk', left_side, right_side, preferred_element_...]
    all_to_all x7 -> x0, waiting for transfers between devices: 34.9 us -> none  [the longest x3 26 us: copy_for_each(): return lax.all_to_all(copies, axis, split_axis=0, concat_axis=0, tiled=True)]
    ppermute x20 -> x0, waiting for transfers between devices: 15.3 us -> none  [from_partner(): return lax.ppermute(value, axis, pairs)]
    select_n x8 -> x0, other arithmetic: 7.15 us -> none  [the longest x2 2.54 us: select_partners(): jnp.where(bits_here == bit_index, fetched[bit_index][1], picked_values)]
    reduce_sum x6 -> x0, other arithmetic: 6.03 us -> none  [the longest x2 4.28 us: per_device(): row_total = row_total + jnp.sum(exponent, axis=-1, keepdims=True)]
  transfers between devices with their start and end apart: 27 -> 0, of which waited for: 9 -> 0; matrix products, arithmetic and copies ran while one was open for 15% -> 0% of each run, Pallas kernels for 0% -> 0%
where the time goes in v1:
time: 114 us
  Pallas kernels  108 us (95%)
  local copies, waits for them, and re-layouts  5.04 us (4%)
    pallas_call x1, Pallas kernels, per_device(): pl.pallas_call(kernel, name='butterfly', out_shape=(jax.ShapeDtypeStruct(...  108 us
    unnamed x13, local copies, waits for them, and re-layouts  5.04 us

profile of v1, /device:TPU:1, one launch (start us, length us, event | category | flops | bytes accessed | tf_op | source)
XLA Modules:
  0.0 114.1 jit_solution(1430213300801792921)
XLA Ops:
  0.6 108.4 %butterfly.1 = (bf16[1024,128]{1,0:T(8,128)(2,1)}, bf16[1024,128]{1,0:T(8,128)(2,1)}, bf16[512,128]{1,0:T(8,128)(2,1)}, bf16[512,128]{1,0:T(8,128)(2,1)}, f32[16,512]{1,0:T(8,128)}) custom-call(s32[1,4]{1,0:T(1,128)} %bits_ref.1, bf16[1024,128]{1,0:T(8,128)(2,1)} %bitcast.10, bf16[512,128]{1,0:T(8,128)(2,1)} %bitcast.14, bf16[512,128]{1,0:T(8,128)(2,1)} %bitcast.15, ...), custom_call_target="tpu_custom_call" | custom-call | tf_op jit(solution)/shard_map/butterfly/pallas_call | solution.py:312
  109.0 0.0 copy-start
  109.0 1.7 %copy.16 = bf16[2,512,128]{2,1,0:T(8,128)(2,1)} copy(bf16[2,512,128]{2,1,0:T(8,128)(2,1)} %bitcast.9) | data formatting | bytes 524288
  110.7 0.0 copy-done
  110.7 0.0 copy-start.2
  110.7 0.7 copy.17
  111.4 0.3 copy-done.2
  111.7 0.0 copy-start.1
  111.7 0.7 copy.18
  112.4 0.3 copy-done.1
  112.7 0.0 copy-start.3
  112.7 0.7 copy.19
  113.3 0.1 copy-done.3
  113.4 0.6 copy.20
Async XLA Ops:
  109.0 1.7 %copy-start = (bf16[1024,128]{1,0:T(8,128)(2,1)S(1)}, bf16[1024,128]{1,0:T(8,128)(2,1)}, u32[]{:S(2)}) copy-start(bf16[1024,128]{1,0:T(8,128)(2,1)} %get-tuple-element.11) | copy-start | bytes 786436
  110.7 1.0 copy-start.2
  111.7 1.0 copy-start.1
  112.7 0.8 copy-start.3

commit v2 on v1

v2 whole, which is shorter than its diff:
```python
import functools
import math

import jax
import jax.numpy as jnp
from jax import lax
from jax.experimental import pallas as pl
from jax.experimental.pallas import tpu as pltpu
from jax.sharding import PartitionSpec as P

MESH = pl.DeviceIdType.MESH
BLOCK = 512
DIM = 128
ROWS = 1024
SUM = 256
CHUNK = 512
SCALE = 1.0 / 12.0
COPIES = 100
EXP2_SCALE = math.log2(math.e) / 12.0
F32, BF16 = jnp.float32, jnp.bfloat16

ORDER = (3, 0, 4, 1, 2)
Z_MASKS = tuple(range(1, 8))
X_MASKS = (8, 16, 24)
HEAD_MASKS = (1, 4, 5, 8, 9, 12, 13)

OWN, SLOT, SUMMARY = 0, 1, 5


def flipped(index, mask):
    out = index
    bit = 1
    while bit <= mask:
        if mask & bit:
            out = out + bit * (1 - 2 * lax.rem(lax.div(index, bit), 2))
        bit *= 2
    return out


def dot(a, b):
    return lax.dot_general(a, b, (((1,), (0,)), ((), ())), preferred_element_type=F32)


def dot_nt(a, b):
    return lax.dot_general(a, b, (((1,), (1,)), ((), ())), preferred_element_type=F32)


def dot_tn(a, b):
    return lax.dot_general(a, b, (((0,), (0,)), ((), ())), preferred_element_type=F32)


def kernel(
    bits_ref, q_ref, k_ref, v_ref, do_ref, proj_ref,
    out_ref, dq_ref, dk_ref, dv_ref, dproj_ref,
    qt, dot_t, part, rx, xsum, zin, half, zbuf, agx,
    kr, vr, ks, vs, e_ref, m_ref, l_ref, mslot, acc, dqt,
    gka, gva, own_gk, own_gv, gslot_k, gslot_v, gk, gv, rgk, rgv,
    part2, rx2, xsum2, zin2, half2, zbuf2, agx2,
    t_ref, rt, w_ref, wb, rh,
    send_sem, recv_sem, edge_sem, hi_sem,
):
    seq = lax.axis_index("seq")
    head = lax.axis_index("head")
    my_x, my_z = lax.div(seq, 8), lax.rem(seq, 8)
    my_y, my_hi, my_core = lax.div(head, 4), lax.rem(lax.div(head, 2), 2), lax.rem(head, 2)
    middle = (my_z == 3) | (my_z == 4)

    barrier = pltpu.get_barrier_semaphore()

    def greet(device):
        pl.semaphore_signal(barrier, inc=1, device_id=device, device_id_type=MESH)

    for mask in (1, 2, 4) + X_MASKS:
        greet({"seq": flipped(seq, mask)})
    for mask in HEAD_MASKS:
        greet({"head": flipped(head, mask)})
    for mask in (3, 5, 6, 7):
        other = flipped(my_z, mask)

        @pl.when(middle | (other == 3) | (other == 4))
        def _():
            greet({"seq": flipped(seq, mask)})

    @pl.when(my_z == 0)
    def _():
        greet({"seq": seq + 7, "head": flipped(head, 2)})

    @pl.when(my_z == 7)
    def _():
        greet({"seq": seq - 7, "head": flipped(head, 2)})

    ids = iter(range(COPIES))
    sent = []

    def start(c):
        c.start()
        sent.append(c)
        return c

    def describe(src, dst, device, n, m):
        return pltpu.make_async_remote_copy(
            src_ref=src, dst_ref=dst, send_sem=send_sem.at[n], recv_sem=recv_sem.at[m],
            device_id=device, device_id_type=MESH,
        )

    def copy(src, dst, axis, mask):
        n = next(ids)
        return start(describe(src, dst, {axis: flipped(seq if axis == "seq" else head, mask)}, n, n))

    def wait_recv(cs):
        for c in cs:
            c.wait_recv()

    proj = proj_ref[...]
    part[0:2] = dot(proj, k_ref[...]).reshape(2, 2, 64, DIM)
    part[2:4] = dot(proj, v_ref[...]).reshape(2, 2, 64, DIM)
    qt[...] = q_ref[...].T
    dot_t[...] = do_ref[...].T

    missing = 10 - (bits_ref[0, 0] + bits_ref[0, 1] + bits_ref[0, 2] + bits_ref[0, 3])
    place = jnp.int32(0)
    for i, b in enumerate(ORDER):
        place = place + jnp.where(missing == b, i, 0)

    at_ends = lax.div(my_z, 7) + lax.div(7 - my_z, 7)
    at_middle = lax.rem(lax.div(my_z + 1, 4), 2) * lax.rem(lax.div(8 - my_z, 4), 2)
    pl.semaphore_wait(barrier, 4 + 3 * at_middle + at_ends + len(X_MASKS) + len(HEAD_MASKS))

    def fetch(i, lo=0, n=BLOCK):
        mask = 1 << ORDER[i]
        return (
            copy(k_ref.at[lo : lo + n], kr.at[i, lo : lo + n], "seq", mask),
            copy(v_ref.at[lo : lo + n], vr.at[i, lo : lo + n], "seq", mask),
        )

    def scatter_x(src, dst):
        return [
            copy(src.at[lax.div(flipped(seq, m), 8)], dst.at[j], "seq", m)
            for j, m in enumerate(X_MASKS)
        ]

    def gather_x(src, dst):
        return [copy(src, dst.at[my_x], "seq", m) for m in X_MASKS]

    def reduce_z(halves, into):
        sends = [next(ids) for _ in range(2)]
        first = [next(ids) for _ in range(7)][0]
        for r in range(2):
            apart = flipped(my_z, 3 + r)

            @pl.when(my_z != 3 + r)
            def _():
                describe(
                    halves.at[r], into.at[apart - 1], {"seq": seq - my_z + (3 + r)}, sends[r], first + apart - 1
                ).start()

        def end():
            for r in range(2):
                @pl.when(my_z != 3 + r)
                def _():
                    describe(halves.at[r], into.at[0], {"seq": flipped(seq, 1)}, sends[r], first).wait_send()

        closing.append(end)
        return first

    def share_z(first, sums, into, buf):
        sends = [next(ids) for _ in range(7)]
        arrive = [next(ids) for _ in range(2)]

        @pl.when(middle)
        def _():
            r = my_z - 3
            total = sums[r]
            for j in range(7):
                describe(buf.at[0], into.at[j], {"seq": flipped(seq, 1)}, sends[0], first + j).wait_recv()
                total = total + into[j].astype(F32)
            buf[r] = total.astype(BF16)
            for j, m in enumerate(Z_MASKS):
                describe(buf.at[r], buf.at[r], {"seq": flipped(seq, m)}, sends[j], arrive[0] + r).start()

        def arrived():
            for r in range(2):
                @pl.when(my_z != 3 + r)
                def _():
                    describe(buf.at[r], buf.at[r], {"seq": flipped(seq, 1)}, sends[0], arrive[r]).wait_recv()

        def end():
            @pl.when(middle)
            def _():
                for j in range(7):
                    describe(buf.at[0], buf.at[0], {"seq": flipped(seq, 1)}, sends[j], arrive[0]).wait_send()

        closing.append(end)
        return arrived

    closing = []

    def forward(row, n, k, v, first=False):
        base = row * BLOCK

        def step(c, carry):
            cols = pl.ds(pl.multiple_of(c * CHUNK, CHUNK), CHUNK)
            s = dot(k[...], qt[:, cols])
            top = jnp.max(s, axis=0, keepdims=True)
            if not first:
                before = m_ref[:, cols]
                top = jnp.maximum(before, top)
                alpha = jnp.exp2((before - top) * EXP2_SCALE)
            e = jnp.exp2((s - top) * EXP2_SCALE)
            total = jnp.sum(e, axis=0, keepdims=True)
            eb = e.astype(BF16)
            e_ref[base : base + n, cols] = eb
            mixed = dot_tn(v[...], eb)
            if not first:
                total = l_ref[:, cols] * alpha + total
                mixed = acc[:, cols] * alpha + mixed
            l_ref[:, cols] = total
            acc[:, cols] = mixed
            m_ref[:, cols] = top
            mslot[row : row + 1, cols] = top
            return carry

        lax.fori_loop(0, ROWS // CHUNK, step, 0)

    def choose(i):
        early = i < place
        ks[i] = jnp.where(early, kr[i], kr[i + 1])
        vs[i] = jnp.where(early, vr[i], vr[i + 1])

    xs = scatter_x(part, rx)
    f_x1 = fetch(0)
    f_x2 = fetch(2)
    f_z4 = fetch(4, 0, 128)
    forward(OWN, BLOCK, k_ref, v_ref, first=True)
    wait_recv(xs)
    xsum[...] = part[my_x] + rx[0] + rx[1] + rx[2]
    half[...] = xsum[...].astype(BF16)
    at_three = reduce_z(half, zin)
    f_z1 = fetch(1)
    gathered = share_z(at_three, xsum, zin, zbuf)
    f_z4 += fetch(4, 128, 128)
    f_z2 = fetch(3)
    f_z4 += fetch(4, 256, 256)
    wait_recv(f_x1 + f_z1)
    choose(0)
    forward(SLOT, BLOCK, ks.at[0], vs.at[0])
    gathered()
    xg = gather_x(zbuf, agx)
    agx[my_x] = zbuf[...]

    @pl.when(my_z == 7)
    def _():
        pl.semaphore_signal(
            edge_sem, inc=1, device_id={"seq": seq - 7, "head": flipped(head, 2)}, device_id_type=MESH
        )

    wait_recv(f_x2)
    choose(1)
    forward(SLOT + 1, BLOCK, ks.at[1], vs.at[1])
    wait_recv(xg)
    sk, sv = ks.at[4, 0:SUM], vs.at[4, 0:SUM]
    sk[...] = agx[0:2].reshape(SUM, DIM)
    sv[...] = agx[2:4].reshape(SUM, DIM)
    forward(SUMMARY, SUM, sk, sv)

    @pl.when(my_z == 0)
    def _():
        pl.semaphore_wait(edge_sem, 1)
        for m in Z_MASKS:
            pl.semaphore_signal(hi_sem, inc=1, device_id={"seq": seq + m}, device_id_type=MESH)

    wait_recv(f_z2)
    choose(2)
    forward(SLOT + 2, BLOCK, ks.at[2], vs.at[2])
    wait_recv(f_z4)
    choose(3)
    forward(SLOT + 3, BLOCK, ks.at[3], vs.at[3])

    inverse = 1.0 / l_ref[...]
    attended = acc[...] * inverse
    delta = jnp.sum(attended * dot_t[...].astype(F32), axis=0, keepdims=True)
    l_ref[...] = inverse
    acc[0:1, :] = delta
    out_ref[...] = attended.T.astype(BF16)
    dqt[...] = jnp.zeros_like(dqt)

    def backward(row, n, k, v, gk_acc, gv_acc):
        base = row * BLOCK
        gk_acc[...] = jnp.zeros_like(gk_acc)
        gv_acc[...] = jnp.zeros_like(gv_acc)

        def step(c, carry):
            cols = pl.ds(pl.multiple_of(c * CHUNK, CHUNK), CHUNK)
            factor = jnp.exp2((mslot[row : row + 1, cols] - m_ref[:, cols]) * EXP2_SCALE) * l_ref[:, cols]
            p = e_ref[base : base + n, cols].astype(F32) * factor
            dp = dot(v[...], dot_t[:, cols])
            ds = (p * (dp - acc[0:1, cols])).astype(BF16)
            dqt[:, cols] += dot_tn(k[...], ds)
            gk_acc[...] += dot(ds, q_ref[cols, :])
            gv_acc[...] += dot(p.astype(BF16), do_ref[cols, :])
            return carry

        lax.fori_loop(0, ROWS // CHUNK, step, 0)

    half_k, half_v = gka.at[0:SUM], gva.at[0:SUM]
    backward(SUMMARY, SUM, sk, sv, half_k, half_v)
    part2[0:2] = (half_k[...] * SCALE).astype(BF16).reshape(2, 2, 64, DIM)
    part2[2:4] = half_v[...].astype(BF16).reshape(2, 2, 64, DIM)
    xs = scatter_x(part2, rx2)

    def slot_back(i):
        backward(SLOT + i, BLOCK, ks.at[i], vs.at[i], gka, gva)
        gslot_k[i] = (gka[...] * SCALE).astype(BF16)
        gslot_v[i] = gva[...].astype(BF16)

    def prepare(i):
        for slots, g in ((gslot_k, gk), (gslot_v, gv)):
            zero = jnp.zeros((BLOCK, DIM), BF16)
            early = slots[i] if i < 4 else zero
            late = slots[i - 1] if i > 0 else zero
            g[i] = jnp.where(i < place, early, jnp.where(i > place, late, zero))

    def give_back(i, lo=0, n=BLOCK):
        mask = 1 << ORDER[i]
        return (
            copy(gk.at[i, lo : lo + n], rgk.at[i, lo : lo + n], "seq", mask),
            copy(gv.at[i, lo : lo + n], rgv.at[i, lo : lo + n], "seq", mask),
        )

    slot_back(3)
    prepare(4)
    wait_recv(xs)
    xsum2[...] = (
        part2[my_x].astype(F32) + rx2[0].astype(F32) + rx2[1].astype(F32) + rx2[2].astype(F32)
    )
    half2[...] = xsum2[...].astype(BF16)
    at_three = reduce_z(half2, zin2)
    r_z4 = give_back(4, 0, 128)
    slot_back(2)
    slot_back(1)
    gathered = share_z(at_three, xsum2, zin2, zbuf2)
    r_z4 += give_back(4, 128, 128)
    prepare(3)
    r_z2 = give_back(3)
    prepare(2)
    r_x2 = give_back(2)
    slot_back(0)
    prepare(0)
    r_x1 = give_back(0)
    prepare(1)
    gathered()
    xg = gather_x(zbuf2, agx2)
    agx2[my_x] = zbuf2[...]
    r_z4 += give_back(4, 256, 128)
    backward(OWN, BLOCK, k_ref, v_ref, own_gk, own_gv)
    wait_recv(xg)
    sg_k = agx2[0:2].reshape(SUM, DIM)
    sg_v = agx2[2:4].reshape(SUM, DIM)
    term = dot_nt(sg_k, k_ref[...]) + dot_nt(sg_v, v_ref[...])
    term = term.astype(BF16).reshape(4, 2, 2, 16, BLOCK)
    t_ref[:, 0] = term[:, :, 0]
    t_ref[:, 1] = term[:, :, 1]

    def term_of(h):
        return t_ref.at[lax.div(h, 4), lax.rem(h, 2)]

    ts = [
        copy(term_of(flipped(head, m)), rt.at[j], "head", m) for j, m in enumerate(HEAD_MASKS)
    ]
    own_gk[...] = own_gk[...] * SCALE + dot_tn(proj_ref[...], sg_k)
    own_gv[...] = own_gv[...] + dot_tn(proj_ref[...], sg_v)
    dq_ref[...] = (dqt[...] * SCALE).T.astype(BF16)
    wait_recv(ts)
    total = t_ref[my_y, my_core].astype(F32)
    for j in range(7):
        total = total + rt[j].astype(F32)
    w_ref[...] = total
    wb[...] = w_ref[1 - my_hi].astype(BF16)

    @pl.when(my_z != 0)
    def _():
        pl.semaphore_wait(hi_sem, 1)

    hs = copy(wb, rh, "head", 2)
    r_z4 += give_back(4, 384, 128)
    r_z1 = give_back(1)
    for c, i in ((r_x1, 0), (r_x2, 2), (r_z2, 3), (r_z1, 1)):
        wait_recv(c)
        own_gk[...] += rgk[i].astype(F32)
        own_gv[...] += rgv[i].astype(F32)
    wait_recv(r_z4)
    dk_ref[...] = (own_gk[...] + rgk[4].astype(F32)).astype(BF16)
    dv_ref[...] = (own_gv[...] + rgv[4].astype(F32)).astype(BF16)
    hs.wait_recv()
    dproj_ref[...] = w_ref[my_hi] + rh[...].astype(F32)
    for c in sent:
        c.wait_send()
    for end in closing:
        end()


def per_device(queries, key_tokens, value_tokens, output_gradient, summary_proj, partner_bits):
    vmem = pl.BlockSpec(memory_space=pltpu.VMEM)
    smem = pl.BlockSpec(memory_space=pltpu.SMEM)
    V = pltpu.VMEM
    out, dq, dk, dv, dproj = pl.pallas_call(
        kernel,
        name="butterfly",
        out_shape=(
            jax.ShapeDtypeStruct((ROWS, DIM), BF16),
            jax.ShapeDtypeStruct((ROWS, DIM), BF16),
            jax.ShapeDtypeStruct((BLOCK, DIM), BF16),
            jax.ShapeDtypeStruct((BLOCK, DIM), BF16),
            jax.ShapeDtypeStruct((16, BLOCK), F32),
        ),
        in_specs=[smem] + [vmem] * 5,
        out_specs=[vmem] * 5,
        scratch_shapes=[
            V((DIM, ROWS), BF16), V((DIM, ROWS), BF16),
            V((4, 2, 64, DIM), F32), V((3, 2, 64, DIM), F32),
            V((2, 64, DIM), F32), V((7, 64, DIM), BF16),
            V((2, 64, DIM), BF16), V((2, 64, DIM), BF16), V((4, 2, 64, DIM), BF16),
            V((5, BLOCK, DIM), BF16), V((5, BLOCK, DIM), BF16),
            V((5, BLOCK, DIM), BF16), V((5, BLOCK, DIM), BF16),
            V((5 * BLOCK + SUM, ROWS), BF16),
            V((1, ROWS), F32), V((1, ROWS), F32), V((8, ROWS), F32),
            V((DIM, ROWS), F32), V((DIM, ROWS), F32),
            V((BLOCK, DIM), F32), V((BLOCK, DIM), F32),
            V((BLOCK, DIM), F32), V((BLOCK, DIM), F32),
            V((4, BLOCK, DIM), BF16), V((4, BLOCK, DIM), BF16),
            V((5, BLOCK, DIM), BF16), V((5, BLOCK, DIM), BF16),
            V((5, BLOCK, DIM), BF16), V((5, BLOCK, DIM), BF16),
            V((4, 2, 64, DIM), BF16), V((3, 2, 64, DIM), BF16),
            V((2, 64, DIM), F32), V((7, 64, DIM), BF16),
            V((2, 64, DIM), BF16), V((2, 64, DIM), BF16), V((4, 2, 64, DIM), BF16),
            V((4, 2, 2, 16, BLOCK), BF16), V((7, 2, 16, BLOCK), BF16),
            V((2, 16, BLOCK), F32), V((16, BLOCK), BF16), V((16, BLOCK), BF16),
            pltpu.SemaphoreType.DMA((COPIES,)), pltpu.SemaphoreType.DMA((COPIES,)),
            pltpu.SemaphoreType.REGULAR, pltpu.SemaphoreType.REGULAR,
        ],
        compiler_params=pltpu.CompilerParams(
            collective_id=0, has_side_effects=True, vmem_limit_bytes=60 * 1024 * 1024
        ),
    )(
        partner_bits,
        queries.reshape(ROWS, DIM),
        key_tokens.reshape(BLOCK, DIM),
        value_tokens.reshape(BLOCK, DIM),
        output_gradient.reshape(ROWS, DIM),
        summary_proj,
    )
    return (
        out.reshape(queries.shape),
        dq.reshape(queries.shape),
        dk.reshape(key_tokens.shape),
        dv.reshape(value_tokens.shape),
        dproj,
    )


def solution(mesh):
    rows = P("head", "seq", None)
    return jax.shard_map(
        per_device,
        mesh=mesh,
        in_specs=(rows, rows, rows, rows, P(None, "seq"), P("seq", None)),
        out_specs=(rows, rows, rows, rows, P("head", "seq")),
        check_vma=False,
    )
```

time: 114 us -> 99.8 us (0.88); the launches traced: 114 us -> 98 us
  Pallas kernels: 108 us -> 92.4 us
    pallas_call x1, Pallas kernels: 108 us -> 92.4 us  [per_device(): pl.pallas_call(kernel, name='butterfly', out_shape=(jax.ShapeDtypeStruct(...]
where the time goes in v2:
time: 99.8 us; the launch traced here: 98 us
  Pallas kernels  92.4 us (93%)
  local copies, waits for them, and re-layouts  5.04 us (5%)
    pallas_call x1, Pallas kernels, per_device(): pl.pallas_call(kernel, name='butterfly', out_shape=(jax.ShapeDtypeStruct(...  92.4 us
    unnamed x13, local copies, waits for them, and re-layouts  5.04 us

profile of v2, /device:TPU:1, one launch (start us, length us, event | category | flops | bytes accessed | tf_op | source)
XLA Modules:
  0.0 98.0 jit_solution(16860444165841524810)
XLA Ops:
  0.6 92.4 %butterfly.1 = (bf16[1024,128]{1,0:T(8,128)(2,1)}, bf16[1024,128]{1,0:T(8,128)(2,1)}, bf16[512,128]{1,0:T(8,128)(2,1)}, bf16[512,128]{1,0:T(8,128)(2,1)}, f32[16,512]{1,0:T(8,128)}) custom-call(s32[1,4]{1,0:T(1,128)} %bits_ref.1, bf16[1024,128]{1,0:T(8,128)(2,1)} %bitcast.10, bf16[512,128]{1,0:T(8,128)(2,1)} %bitcast.14, bf16[512,128]{1,0:T(8,128)(2,1)} %bitcast.15, ...), custom_call_target="tpu_custom_call" | custom-call | tf_op jit(solution)/shard_map/butterfly/pallas_call | solution.py:406
  93.0 0.0 copy-start
  93.0 1.7 %copy.16 = bf16[2,512,128]{2,1,0:T(8,128)(2,1)} copy(bf16[2,512,128]{2,1,0:T(8,128)(2,1)} %bitcast.9) | data formatting | bytes 524288
  94.7 0.0 copy-done
  94.7 0.0 copy-start.2
  94.7 0.7 copy.17
  95.4 0.3 copy-done.2
  95.7 0.0 copy-start.1
  95.7 0.7 copy.18
  96.4 0.3 copy-done.1
  96.7 0.0 copy-start.3
  96.7 0.7 copy.19
  97.3 0.1 copy-done.3
  97.4 0.6 copy.20
Async XLA Ops:
  93.0 1.7 %copy-start = (bf16[1024,128]{1,0:T(8,128)(2,1)S(1)}, bf16[1024,128]{1,0:T(8,128)(2,1)}, u32[]{:S(2)}) copy-start(bf16[1024,128]{1,0:T(8,128)(2,1)} %get-tuple-element.11) | copy-start | bytes 786436
  94.7 1.0 %copy-start.2 = (bf16[512,128]{1,0:T(8,128)(2,1)S(1)}, bf16[512,128]{1,0:T(8,128)(2,1)}, u32[]{:S(2)}) copy-start(bf16[512,128]{1,0:T(8,128)(2,1)} %get-tuple-element.12) | copy-start | bytes 393220
  95.7 1.0 copy-start.1
  96.7 0.8 copy-start.3

commit v3 on v2

--- a/solution.py
+++ b/solution.py
@@ -15,9 +15,13 @@
 SUM = 256
 CHUNK = 512
 SCALE = 1.0 / 12.0
-COPIES = 100
+COPIES = 120
 EXP2_SCALE = math.log2(math.e) / 12.0
 F32, BF16 = jnp.float32, jnp.bfloat16
+
+LAST = {0: 4, 1: 5, 2: 6, 3: 7, 4: 6, 5: 7, 6: 7}
+RELAY_IN = {s: [z for z in range(s, 8) if LAST[z - s] >= z] for s in (1, 2, 3, 4)}
+RELAY_OUT = {s: [z - 1 for z in RELAY_IN[s]] for s in (1, 2, 3, 4)}
 
 ORDER = (3, 0, 4, 1, 2)
 Z_MASKS = tuple(range(1, 8))
@@ -53,11 +57,11 @@
     bits_ref, q_ref, k_ref, v_ref, do_ref, proj_ref,
     out_ref, dq_ref, dk_ref, dv_ref, dproj_ref,
     qt, dot_t, part, rx, xsum, zin, half, zbuf, agx,
-    kr, vr, ks, vs, e_ref, m_ref, l_ref, mslot, acc, dqt,
-    gka, gva, own_gk, own_gv, gslot_k, gslot_v, gk, gv, rgk, rgv,
+    kx, vx, kz, vz, ks, vs, e_ref, m_ref, l_ref, mslot, acc, dqt,
+    gka, gva, own_gk, own_gv, gslot_k, gslot_v, gk, gv, rgk, rgv, zsk, zsv, zrk, zrv,
     part2, rx2, xsum2, zin2, half2, zbuf2, agx2,
     t_ref, rt, w_ref, wb, rh,
-    send_sem, recv_sem, edge_sem, hi_sem,
+    send_sem, recv_sem, near_sem, edge_sem, hi_sem,
 ):
     seq = lax.axis_index("seq")
     head = lax.axis_index("head")
@@ -70,16 +74,18 @@
     def greet(device):
         pl.semaphore_signal(barrier, inc=1, device_id=device, device_id_type=MESH)
 
-    for mask in (1, 2, 4) + X_MASKS:
+    for mask in X_MASKS:
         greet({"seq": flipped(seq, mask)})
     for mask in HEAD_MASKS:
         greet({"head": flipped(head, mask)})
-    for mask in (3, 5, 6, 7):
-        other = flipped(my_z, mask)
-
-        @pl.when(middle | (other == 3) | (other == 4))
-        def _():
-            greet({"seq": flipped(seq, mask)})
+
+    @pl.when(my_z < 7)
+    def _():
+        greet({"seq": seq + 1})
+
+    @pl.when(my_z > 0)
+    def _():
+        greet({"seq": seq - 1})
 
     @pl.when(my_z == 0)
     def _():
@@ -89,6 +95,14 @@
     def _():
         greet({"seq": seq - 7, "head": flipped(head, 2)})
 
+    def one_of(places, mirrored=False):
+        found = None
+        for z in places:
+            here = my_z == (7 - z if mirrored else z)
+            found = here if found is None else found | here
+        return found
+
+    closing = []
     ids = iter(range(COPIES))
     sent = []
 
@@ -122,16 +136,73 @@
     for i, b in enumerate(ORDER):
         place = place + jnp.where(missing == b, i, 0)
 
-    at_ends = lax.div(my_z, 7) + lax.div(7 - my_z, 7)
-    at_middle = lax.rem(lax.div(my_z + 1, 4), 2) * lax.rem(lax.div(8 - my_z, 4), 2)
-    pl.semaphore_wait(barrier, 4 + 3 * at_middle + at_ends + len(X_MASKS) + len(HEAD_MASKS))
-
-    def fetch(i, lo=0, n=BLOCK):
-        mask = 1 << ORDER[i]
+    pl.semaphore_wait(barrier, 2 + len(X_MASKS) + len(HEAD_MASKS))
+
+    def tell(n):
+        for way, there in ((0, my_z < 7), (1, my_z > 0)):
+            @pl.when(there)
+            def _():
+                pl.semaphore_signal(
+                    near_sem.at[2 * n + way], inc=1, device_id={"seq": seq + 1 - 2 * way}, device_id_type=MESH
+                )
+
+    def hear(n):
+        for way, there in ((0, my_z > 0), (1, my_z < 7)):
+            @pl.when(there)
+            def _():
+                pl.semaphore_wait(near_sem.at[2 * n + way], 1)
+
+    def fetch(j, mask):
         return (
-            copy(k_ref.at[lo : lo + n], kr.at[i, lo : lo + n], "seq", mask),
-            copy(v_ref.at[lo : lo + n], vr.at[i, lo : lo + n], "seq", mask),
+            copy(k_ref, kx.at[j], "seq", mask),
+            copy(v_ref, vx.at[j], "seq", mask),
         )
+
+    def relay(source, into, n):
+        pieces = []
+        for way in (0, 1):
+            i = next(ids)
+            device = {"seq": seq + 1 - 2 * way}
+            pieces.append((way, i, device))
+
+        def c(way, i, device):
+            return describe(source(way), into(way), device, i, i)
+
+        def go(senders):
+            for way, i, device in pieces:
+                @pl.when(one_of(senders, way == 1))
+                def _():
+                    c(way, i, device).start()
+
+            def end():
+                for way, i, device in pieces:
+                    @pl.when(one_of(senders, way == 1))
+                    def _():
+                        c(way, i, device).wait_send()
+
+            closing.append(end)
+
+        def arrived(receivers):
+            for way, i, device in pieces:
+                @pl.when(one_of(receivers, way == 1))
+                def _():
+                    c(way, i, device).wait_recv()
+
+        return go, arrived
+
+    def fetch_z(own, into):
+        steps = []
+        for n in (1, 2, 3, 4):
+            source = (lambda way: own) if n == 1 else (lambda way, n=n: into.at[way, n - 2])
+            steps.append(relay(source, lambda way, n=n: into.at[way, n - 1], n))
+
+        def go(n):
+            if n > 1:
+                steps[n - 2][1](RELAY_IN[n - 1])
+            if n <= 4:
+                steps[n - 1][0](RELAY_OUT[n])
+
+        return go
 
     def scatter_x(src, dst):
         return [
@@ -192,8 +263,6 @@
 
         closing.append(end)
         return arrived
-
-    closing = []
 
     def forward(row, n, k, v, first=False):
         base = row * BLOCK
@@ -222,31 +291,54 @@
 
         lax.fori_loop(0, ROWS // CHUNK, step, 0)
 
+    from_above = [1 - lax.rem(lax.div(my_z, b), 2) for b in (1, 2, 4)]
+
+    def partner(i, x, z):
+        if ORDER[i] >= 3:
+            return x[ORDER[i] - 3]
+        bit = ORDER[i]
+        return z[from_above[bit], (1 << bit) - 1]
+
     def choose(i):
         early = i < place
-        ks[i] = jnp.where(early, kr[i], kr[i + 1])
-        vs[i] = jnp.where(early, vr[i], vr[i + 1])
-
+        ks[i] = jnp.where(early, partner(i, kx, kz), partner(i + 1, kx, kz))
+        vs[i] = jnp.where(early, partner(i, vx, vz), partner(i + 1, vx, vz))
+
+    go_k, go_v = fetch_z(k_ref, kz), fetch_z(v_ref, vz)
+    go_k(1)
+    go_v(1)
+    tell(0)
     xs = scatter_x(part, rx)
-    f_x1 = fetch(0)
-    f_x2 = fetch(2)
-    f_z4 = fetch(4, 0, 128)
+    f_x1 = fetch(0, 8)
+    f_x2 = fetch(1, 16)
     forward(OWN, BLOCK, k_ref, v_ref, first=True)
+    hear(0)
+    tell(1)
+    go_k(2)
+    hear(1)
+    tell(2)
     wait_recv(xs)
     xsum[...] = part[my_x] + rx[0] + rx[1] + rx[2]
     half[...] = xsum[...].astype(BF16)
+    hear(2)
     at_three = reduce_z(half, zin)
-    f_z1 = fetch(1)
-    gathered = share_z(at_three, xsum, zin, zbuf)
-    f_z4 += fetch(4, 128, 128)
-    f_z2 = fetch(3)
-    f_z4 += fetch(4, 256, 256)
-    wait_recv(f_x1 + f_z1)
+    go_v(2)
+    wait_recv(f_x1)
     choose(0)
     forward(SLOT, BLOCK, ks.at[0], vs.at[0])
+    go_k(3)
+    gathered = share_z(at_three, xsum, zin, zbuf)
+    go_v(3)
+    wait_recv(f_x2)
+    choose(1)
+    forward(SLOT + 1, BLOCK, ks.at[1], vs.at[1])
+    go_k(4)
     gathered()
     xg = gather_x(zbuf, agx)
     agx[my_x] = zbuf[...]
+    go_v(4)
+    choose(2)
+    forward(SLOT + 2, BLOCK, ks.at[2], vs.at[2])
 
     @pl.when(my_z == 7)
     def _():
@@ -254,9 +346,6 @@
             edge_sem, inc=1, device_id={"seq": seq - 7, "head": flipped(head, 2)}, device_id_type=MESH
         )
 
-    wait_recv(f_x2)
-    choose(1)
-    forward(SLOT + 1, BLOCK, ks.at[1], vs.at[1])
     wait_recv(xg)
     sk, sv = ks.at[4, 0:SUM], vs.at[4, 0:SUM]
     sk[...] = agx[0:2].reshape(SUM, DIM)
@@ -269,10 +358,8 @@
         for m in Z_MASKS:
             pl.semaphore_signal(hi_sem, inc=1, device_id={"seq": seq + m}, device_id_type=MESH)
 
-    wait_recv(f_z2)
-    choose(2)
-    forward(SLOT + 2, BLOCK, ks.at[2], vs.at[2])
-    wait_recv(f_z4)
+    go_k(5)
+    go_v(5)
     choose(3)
     forward(SLOT + 3, BLOCK, ks.at[3], vs.at[3])
 
@@ -320,39 +407,73 @@
             late = slots[i - 1] if i > 0 else zero
             g[i] = jnp.where(i < place, early, jnp.where(i > place, late, zero))
 
-    def give_back(i, lo=0, n=BLOCK):
-        mask = 1 << ORDER[i]
+    def give_back(j, i, mask):
         return (
-            copy(gk.at[i, lo : lo + n], rgk.at[i, lo : lo + n], "seq", mask),
-            copy(gv.at[i, lo : lo + n], rgv.at[i, lo : lo + n], "seq", mask),
+            copy(gk.at[i], rgk.at[j], "seq", mask),
+            copy(gv.at[i], rgv.at[j], "seq", mask),
         )
 
+    def return_z(g, sums, into):
+        steps = {}
+        for n in (4, 3, 2, 1):
+            if n == 4:
+                source = lambda way: g.at[4]
+            elif n == 3:
+                source = lambda way: into.at[way, 3]
+            else:
+                source = lambda way, n=n: sums.at[way, n - 1]
+            steps[n] = relay(source, lambda way, n=n: into.at[way, n - 1], n)
+
+        def up_down(places):
+            return [7 - z for z in places]
+
+        def go(n):
+            if n < 4:
+                steps[n + 1][1](up_down(RELAY_OUT[n + 1]))
+            if n in (1, 2):
+                own_value = g[3 if n == 2 else 1].astype(F32)
+                for way in (0, 1):
+                    came = one_of(up_down(RELAY_OUT[n + 1]), way == 1)
+                    mine = from_above[n - 1] == 1 - way
+                    sums[way, n - 1] = (
+                        jnp.where(came, into[way, n].astype(F32), 0.0) + jnp.where(mine, own_value, 0.0)
+                    ).astype(BF16)
+            if n > 0:
+                steps[n][0](up_down(RELAY_IN[n]))
+
+        return go
+
+    back_k, back_v = return_z(gk, zsk, zrk), return_z(gv, zsv, zrv)
     slot_back(3)
     prepare(4)
+    back_k(4)
+    slot_back(2)
+    prepare(3)
     wait_recv(xs)
     xsum2[...] = (
         part2[my_x].astype(F32) + rx2[0].astype(F32) + rx2[1].astype(F32) + rx2[2].astype(F32)
     )
     half2[...] = xsum2[...].astype(BF16)
     at_three = reduce_z(half2, zin2)
-    r_z4 = give_back(4, 0, 128)
-    slot_back(2)
+    back_v(4)
     slot_back(1)
-    gathered = share_z(at_three, xsum2, zin2, zbuf2)
-    r_z4 += give_back(4, 128, 128)
-    prepare(3)
-    r_z2 = give_back(3)
     prepare(2)
-    r_x2 = give_back(2)
+    r_x2 = give_back(1, 2, 16)
+    back_k(3)
     slot_back(0)
     prepare(0)
-    r_x1 = give_back(0)
+    r_x1 = give_back(0, 0, 8)
     prepare(1)
+    gathered = share_z(at_three, xsum2, zin2, zbuf2)
+    back_v(3)
+    back_k(2)
+    backward(OWN, BLOCK, k_ref, v_ref, own_gk, own_gv)
+    back_v(2)
     gathered()
     xg = gather_x(zbuf2, agx2)
     agx2[my_x] = zbuf2[...]
-    r_z4 += give_back(4, 256, 128)
-    backward(OWN, BLOCK, k_ref, v_ref, own_gk, own_gv)
+    dq_ref[...] = (dqt[...] * SCALE).T.astype(BF16)
+    back_k(1)
     wait_recv(xg)
     sg_k = agx2[0:2].reshape(SUM, DIM)
     sg_v = agx2[2:4].reshape(SUM, DIM)
@@ -369,7 +490,7 @@
     ]
     own_gk[...] = own_gk[...] * SCALE + dot_tn(proj_ref[...], sg_k)
     own_gv[...] = own_gv[...] + dot_tn(proj_ref[...], sg_v)
-    dq_ref[...] = (dqt[...] * SCALE).T.astype(BF16)
+    back_v(1)
     wait_recv(ts)
     total = t_ref[my_y, my_core].astype(F32)
     for j in range(7):
@@ -382,15 +503,18 @@
         pl.semaphore_wait(hi_sem, 1)
 
     hs = copy(wb, rh, "head", 2)
-    r_z4 += give_back(4, 384, 128)
-    r_z1 = give_back(1)
-    for c, i in ((r_x1, 0), (r_x2, 2), (r_z2, 3), (r_z1, 1)):
+    for c, j in ((r_x1, 0), (r_x2, 1)):
         wait_recv(c)
-        own_gk[...] += rgk[i].astype(F32)
-        own_gv[...] += rgv[i].astype(F32)
-    wait_recv(r_z4)
-    dk_ref[...] = (own_gk[...] + rgk[4].astype(F32)).astype(BF16)
-    dv_ref[...] = (own_gv[...] + rgv[4].astype(F32)).astype(BF16)
+        own_gk[...] += rgk[j].astype(F32)
+        own_gv[...] += rgv[j].astype(F32)
+    up_arrives, down_arrives = my_z > 0, my_z < 7
+    for back, own, into, result in ((back_k, own_gk, zrk, dk_ref), (back_v, own_gv, zrv, dv_ref)):
+        back(0)
+        result[...] = (
+            own[...]
+            + jnp.where(up_arrives, into[0, 0].astype(F32), 0.0)
+            + jnp.where(down_arrives, into[1, 0].astype(F32), 0.0)
+        ).astype(BF16)
     hs.wait_recv()
     dproj_ref[...] = w_ref[my_hi] + rh[...].astype(F32)
     for c in sent:
@@ -407,11 +531,11 @@
         kernel,
         name="butterfly",
         out_shape=(
-            jax.ShapeDtypeStruct((ROWS, DIM), BF16),
-            jax.ShapeDtypeStruct((ROWS, DIM), BF16),
-            jax.ShapeDtypeStruct((BLOCK, DIM), BF16),
-            jax.ShapeDtypeStruct((BLOCK, DIM), BF16),
-            jax.ShapeDtypeStruct((16, BLOCK), F32),
+            pltpu.VMEM((ROWS, DIM), BF16),
+            pltpu.VMEM((ROWS, DIM), BF16),
+            pltpu.VMEM((BLOCK, DIM), BF16),
+            pltpu.VMEM((BLOCK, DIM), BF16),
+            pltpu.VMEM((16, BLOCK), F32),
         ),
         in_specs=[smem] + [vmem] * 5,
         out_specs=[vmem] * 5,
@@ -420,7 +544,8 @@
             V((4, 2, 64, DIM), F32), V((3, 2, 64, DIM), F32),
             V((2, 64, DIM), F32), V((7, 64, DIM), BF16),
             V((2, 64, DIM), BF16), V((2, 64, DIM), BF16), V((4, 2, 64, DIM), BF16),
-            V((5, BLOCK, DIM), BF16), V((5, BLOCK, DIM), BF16),
+            V((2, BLOCK, DIM), BF16), V((2, BLOCK, DIM), BF16),
+            V((2, 4, BLOCK, DIM), BF16), V((2, 4, BLOCK, DIM), BF16),
             V((5, BLOCK, DIM), BF16), V((5, BLOCK, DIM), BF16),
             V((5 * BLOCK + SUM, ROWS), BF16),
             V((1, ROWS), F32), V((1, ROWS), F32), V((8, ROWS), F32),
@@ -429,14 +554,16 @@
             V((BLOCK, DIM), F32), V((BLOCK, DIM), F32),
             V((4, BLOCK, DIM), BF16), V((4, BLOCK, DIM), BF16),
             V((5, BLOCK, DIM), BF16), V((5, BLOCK, DIM), BF16),
-            V((5, BLOCK, DIM), BF16), V((5, BLOCK, DIM), BF16),
+            V((2, BLOCK, DIM), BF16), V((2, BLOCK, DIM), BF16),
+            V((2, 2, BLOCK, DIM), BF16), V((2, 2, BLOCK, DIM), BF16),
+            V((2, 4, BLOCK, DIM), BF16), V((2, 4, BLOCK, DIM), BF16),
             V((4, 2, 64, DIM), BF16), V((3, 2, 64, DIM), BF16),
             V((2, 64, DIM), F32), V((7, 64, DIM), BF16),
             V((2, 64, DIM), BF16), V((2, 64, DIM), BF16), V((4, 2, 64, DIM), BF16),
             V((4, 2, 2, 16, BLOCK), BF16), V((7, 2, 16, BLOCK), BF16),
             V((2, 16, BLOCK), F32), V((16, BLOCK), BF16), V((16, BLOCK), BF16),
             pltpu.SemaphoreType.DMA((COPIES,)), pltpu.SemaphoreType.DMA((COPIES,)),
-            pltpu.SemaphoreType.REGULAR, pltpu.SemaphoreType.REGULAR,
+            pltpu.SemaphoreType.REGULAR((6,)), pltpu.SemaphoreType.REGULAR, pltpu.SemaphoreType.REGULAR,
         ],
         compiler_params=pltpu.CompilerParams(
             collective_id=0, has_side_effects=True, vmem_limit_bytes=60 * 1024 * 1024

time: 99.8 us -> 83.8 us (0.84); the launches traced: 98 us -> 83.7 us
  Pallas kernels: 92.4 us -> 79.7 us
  local copies, waits for them, and re-layouts: 5.04 us -> 3.33 us
    pallas_call x1, Pallas kernels: 92.4 us -> 79.7 us  [per_device(): pl.pallas_call(kernel, name='butterfly', out_shape=(pltpu.VMEM((ROWS, DIM...]
    unnamed x13 -> x5, local copies, waits for them, and re-layouts: 5.04 us -> 3.33 us
where the time goes in v3:
time: 83.8 us; the launch traced here: 83.7 us
  Pallas kernels  79.7 us (95%)
  local copies, waits for them, and re-layouts  3.33 us (4%)
    pallas_call x1, Pallas kernels, per_device(): pl.pallas_call(kernel, name='butterfly', out_shape=(pltpu.VMEM((ROWS, DIM...  79.7 us
    unnamed x5, local copies, waits for them, and re-layouts  3.33 us

profile of v3, /device:TPU:1, one launch (start us, length us, event | category | flops | bytes accessed | tf_op | source)
XLA Modules:
  0.0 83.7 jit_solution(8701599646810251584)
XLA Ops:
  0.6 79.7 %butterfly.1 = (bf16[1024,128]{1,0:T(8,128)(2,1)S(1)}, bf16[1024,128]{1,0:T(8,128)(2,1)S(1)}, bf16[512,128]{1,0:T(8,128)(2,1)S(1)}, bf16[512,128]{1,0:T(8,128)(2,1)S(1)}, f32[16,512]{1,0:T(8,128)S(1)}) custom-call(s32[1,4]{1,0:T(1,128)} %bits_ref.1, bf16[1024,128]{1,0:T(8,128)(2,1)} %bitcast.12, bf16[512,128]{1,0:T(8,128)(2,1)} %bitcast.14, ...), custom_call_target="tpu_custom_call" | custom-call | tf_op jit(solution)/shard_map/butterfly/pallas_call | solution.py:530
  80.4 0.7 copy.16
  81.1 0.7 copy.17
  81.8 0.6 copy.20
  82.4 0.7 copy.18
  83.0 0.7 copy.19

commit v4 on v3

--- a/solution.py
+++ b/solution.py
@@ -54,13 +54,14 @@
 
 
 def kernel(
-    bits_ref, q_ref, k_ref, v_ref, do_ref, proj_ref,
+    bits_ref, q_in, k_in, v_in, do_in, proj_in,
     out_ref, dq_ref, dk_ref, dv_ref, dproj_ref,
+    q_ref, k_ref, v_ref, do_ref, proj_ref, load_sem,
     qt, dot_t, part, rx, xsum, zin, half, zbuf, agx,
-    kx, vx, kz, vz, ks, vs, e_ref, m_ref, l_ref, mslot, acc, dqt,
+    kx, vx, kz, vz, ks, vs, e_ref, m_ref, l_ref, mslot, rescale, delta_ref, acc, dqt,
     gka, gva, own_gk, own_gv, gslot_k, gslot_v, gk, gv, rgk, rgv, zsk, zsv, zrk, zrv,
     part2, rx2, xsum2, zin2, half2, zbuf2, agx2,
-    t_ref, rt, w_ref, wb, rh,
+    t_ref, rt, rt2, w_ref, wb, rh,
     send_sem, recv_sem, near_sem, edge_sem, hi_sem,
 ):
     seq = lax.axis_index("seq")
@@ -95,6 +96,15 @@
     def _():
         greet({"seq": seq - 7, "head": flipped(head, 2)})
 
+    loads = [
+        pltpu.make_async_copy(src, dst, load_sem.at[n])
+        for n, (src, dst) in enumerate(
+            ((k_in, k_ref), (v_in, v_ref), (proj_in, proj_ref), (q_in, q_ref), (do_in, do_ref))
+        )
+    ]
+    for load in loads:
+        load.start()
+
     def one_of(places, mirrored=False):
         found = None
         for z in places:
@@ -125,9 +135,14 @@
         for c in cs:
             c.wait_recv()
 
+    for load in loads[:3]:
+        load.wait()
+
     proj = proj_ref[...]
     part[0:2] = dot(proj, k_ref[...]).reshape(2, 2, 64, DIM)
     part[2:4] = dot(proj, v_ref[...]).reshape(2, 2, 64, DIM)
+    for load in loads[3:]:
+        load.wait()
     qt[...] = q_ref[...].T
     dot_t[...] = do_ref[...].T
 
@@ -264,7 +279,7 @@
         closing.append(end)
         return arrived
 
-    def forward(row, n, k, v, first=False):
+    def scores(row, n, k, first=False):
         base = row * BLOCK
 
         def step(c, carry):
@@ -275,21 +290,35 @@
                 before = m_ref[:, cols]
                 top = jnp.maximum(before, top)
                 alpha = jnp.exp2((before - top) * EXP2_SCALE)
+                rescale[:, cols] = alpha
             e = jnp.exp2((s - top) * EXP2_SCALE)
             total = jnp.sum(e, axis=0, keepdims=True)
-            eb = e.astype(BF16)
-            e_ref[base : base + n, cols] = eb
-            mixed = dot_tn(v[...], eb)
+            e_ref[base : base + n, cols] = e.astype(BF16)
             if not first:
                 total = l_ref[:, cols] * alpha + total
-                mixed = acc[:, cols] * alpha + mixed
             l_ref[:, cols] = total
-            acc[:, cols] = mixed
             m_ref[:, cols] = top
             mslot[row : row + 1, cols] = top
             return carry
 
         lax.fori_loop(0, ROWS // CHUNK, step, 0)
+
+    def mix(row, n, v, first=False):
+        base = row * BLOCK
+
+        def step(c, carry):
+            cols = pl.ds(pl.multiple_of(c * CHUNK, CHUNK), CHUNK)
+            mixed = dot_tn(v[...], e_ref[base : base + n, cols])
+            if not first:
+                mixed = acc[:, cols] * rescale[:, cols] + mixed
+            acc[:, cols] = mixed
+            return carry
+
+        lax.fori_loop(0, ROWS // CHUNK, step, 0)
+
+    def forward(row, n, k, v, first=False):
+        scores(row, n, k, first)
+        mix(row, n, v, first)
 
     from_above = [1 - lax.rem(lax.div(my_z, b), 2) for b in (1, 2, 4)]
 
@@ -299,10 +328,8 @@
         bit = ORDER[i]
         return z[from_above[bit], (1 << bit) - 1]
 
-    def choose(i):
-        early = i < place
-        ks[i] = jnp.where(early, partner(i, kx, kz), partner(i + 1, kx, kz))
-        vs[i] = jnp.where(early, partner(i, vx, vz), partner(i + 1, vx, vz))
+    def choose(i, chosen, x, z):
+        chosen[i] = jnp.where(i < place, partner(i, x, z), partner(i + 1, x, z))
 
     go_k, go_v = fetch_z(k_ref, kz), fetch_z(v_ref, vz)
     go_k(1)
@@ -324,20 +351,23 @@
     at_three = reduce_z(half, zin)
     go_v(2)
     wait_recv(f_x1)
-    choose(0)
+    choose(0, ks, kx, kz)
+    choose(0, vs, vx, vz)
     forward(SLOT, BLOCK, ks.at[0], vs.at[0])
     go_k(3)
     gathered = share_z(at_three, xsum, zin, zbuf)
     go_v(3)
     wait_recv(f_x2)
-    choose(1)
+    choose(1, ks, kx, kz)
+    choose(1, vs, vx, vz)
     forward(SLOT + 1, BLOCK, ks.at[1], vs.at[1])
     go_k(4)
     gathered()
     xg = gather_x(zbuf, agx)
     agx[my_x] = zbuf[...]
     go_v(4)
-    choose(2)
+    choose(2, ks, kx, kz)
+    choose(2, vs, vx, vz)
     forward(SLOT + 2, BLOCK, ks.at[2], vs.at[2])
 
     @pl.when(my_z == 7)
@@ -346,6 +376,7 @@
             edge_sem, inc=1, device_id={"seq": seq - 7, "head": flipped(head, 2)}, device_id_type=MESH
         )
 
+    dqt[...] = jnp.zeros_like(dqt)
     wait_recv(xg)
     sk, sv = ks.at[4, 0:SUM], vs.at[4, 0:SUM]
     sk[...] = agx[0:2].reshape(SUM, DIM)
@@ -359,17 +390,15 @@
             pl.semaphore_signal(hi_sem, inc=1, device_id={"seq": seq + m}, device_id_type=MESH)
 
     go_k(5)
+    choose(3, ks, kx, kz)
+    scores(SLOT + 3, BLOCK, ks.at[3])
+    l_ref[...] = 1.0 / l_ref[...]
     go_v(5)
-    choose(3)
-    forward(SLOT + 3, BLOCK, ks.at[3], vs.at[3])
-
-    inverse = 1.0 / l_ref[...]
-    attended = acc[...] * inverse
-    delta = jnp.sum(attended * dot_t[...].astype(F32), axis=0, keepdims=True)
-    l_ref[...] = inverse
-    acc[0:1, :] = delta
-    out_ref[...] = attended.T.astype(BF16)
-    dqt[...] = jnp.zeros_like(dqt)
+    choose(3, vs, vx, vz)
+    mix(SLOT + 3, BLOCK, vs.at[3])
+
+    attended = acc[...] * l_ref[...]
+    delta_ref[...] = jnp.sum(attended * dot_t[...].astype(F32), axis=0, keepdims=True)
 
     def backward(row, n, k, v, gk_acc, gv_acc):
         base = row * BLOCK
@@ -381,7 +410,7 @@
             factor = jnp.exp2((mslot[row : row + 1, cols] - m_ref[:, cols]) * EXP2_SCALE) * l_ref[:, cols]
             p = e_ref[base : base + n, cols].astype(F32) * factor
             dp = dot(v[...], dot_t[:, cols])
-            ds = (p * (dp - acc[0:1, cols])).astype(BF16)
+            ds = (p * (dp - delta_ref[:, cols])).astype(BF16)
             dqt[:, cols] += dot_tn(k[...], ds)
             gk_acc[...] += dot(ds, q_ref[cols, :])
             gv_acc[...] += dot(p.astype(BF16), do_ref[cols, :])
@@ -407,11 +436,8 @@
             late = slots[i - 1] if i > 0 else zero
             g[i] = jnp.where(i < place, early, jnp.where(i > place, late, zero))
 
-    def give_back(j, i, mask):
-        return (
-            copy(gk.at[i], rgk.at[j], "seq", mask),
-            copy(gv.at[i], rgv.at[j], "seq", mask),
-        )
+    def give_back(g, into, j, i, mask):
+        return copy(g.at[i], into.at[j], "seq", mask)
 
     def return_z(g, sums, into):
         steps = {}
@@ -444,36 +470,36 @@
         return go
 
     back_k, back_v = return_z(gk, zsk, zrk), return_z(gv, zsv, zrv)
+    out_ref[...] = (acc[...] * l_ref[...]).T.astype(BF16)
     slot_back(3)
     prepare(4)
-    back_k(4)
-    slot_back(2)
-    prepare(3)
     wait_recv(xs)
     xsum2[...] = (
         part2[my_x].astype(F32) + rx2[0].astype(F32) + rx2[1].astype(F32) + rx2[2].astype(F32)
     )
     half2[...] = xsum2[...].astype(BF16)
     at_three = reduce_z(half2, zin2)
+    back_k(4)
     back_v(4)
+    slot_back(2)
+    prepare(3)
     slot_back(1)
     prepare(2)
-    r_x2 = give_back(1, 2, 16)
-    back_k(3)
+    r_x2 = [give_back(gk, rgk, 1, 2, 16)]
     slot_back(0)
     prepare(0)
-    r_x1 = give_back(0, 0, 8)
+    r_x1 = [give_back(gk, rgk, 0, 0, 8)]
     prepare(1)
     gathered = share_z(at_three, xsum2, zin2, zbuf2)
+    back_k(3)
+    backward(OWN, BLOCK, k_ref, v_ref, own_gk, own_gv)
     back_v(3)
-    back_k(2)
-    backward(OWN, BLOCK, k_ref, v_ref, own_gk, own_gv)
-    back_v(2)
     gathered()
     xg = gather_x(zbuf2, agx2)
     agx2[my_x] = zbuf2[...]
+    back_k(2)
+    back_v(2)
     dq_ref[...] = (dqt[...] * SCALE).T.astype(BF16)
-    back_k(1)
     wait_recv(xg)
     sg_k = agx2[0:2].reshape(SUM, DIM)
     sg_v = agx2[2:4].reshape(SUM, DIM)
@@ -482,27 +508,38 @@
     t_ref[:, 0] = term[:, :, 0]
     t_ref[:, 1] = term[:, :, 1]
 
-    def term_of(h):
-        return t_ref.at[lax.div(h, 4), lax.rem(h, 2)]
-
-    ts = [
-        copy(term_of(flipped(head, m)), rt.at[j], "head", m) for j, m in enumerate(HEAD_MASKS)
-    ]
+    def exchange(hi, into):
+        return [
+            copy(
+                t_ref.at[lax.div(flipped(head, m), 4), lax.rem(flipped(head, m), 2), hi], into.at[j], "head", m
+            )
+            for j, m in enumerate(HEAD_MASKS)
+        ]
+
+    def summed(hi, arrived):
+        total = t_ref[my_y, my_core, hi].astype(F32)
+        for j in range(7):
+            total = total + arrived[j].astype(F32)
+        return total
+
+    first = exchange(1 - my_hi, rt)
+    second = exchange(my_hi, rt2)
+    r_x2.append(give_back(gv, rgv, 1, 2, 16))
+    r_x1.append(give_back(gv, rgv, 0, 0, 8))
     own_gk[...] = own_gk[...] * SCALE + dot_tn(proj_ref[...], sg_k)
     own_gv[...] = own_gv[...] + dot_tn(proj_ref[...], sg_v)
-    back_v(1)
-    wait_recv(ts)
-    total = t_ref[my_y, my_core].astype(F32)
-    for j in range(7):
-        total = total + rt[j].astype(F32)
-    w_ref[...] = total
-    wb[...] = w_ref[1 - my_hi].astype(BF16)
+    wait_recv(first)
+    wb[...] = summed(1 - my_hi, rt).astype(BF16)
 
     @pl.when(my_z != 0)
     def _():
         pl.semaphore_wait(hi_sem, 1)
 
     hs = copy(wb, rh, "head", 2)
+    back_k(1)
+    back_v(1)
+    wait_recv(second)
+    w_ref[...] = summed(my_hi, rt2)
     for c, j in ((r_x1, 0), (r_x2, 1)):
         wait_recv(c)
         own_gk[...] += rgk[j].astype(F32)
@@ -516,11 +553,20 @@
             + jnp.where(down_arrives, into[1, 0].astype(F32), 0.0)
         ).astype(BF16)
     hs.wait_recv()
-    dproj_ref[...] = w_ref[my_hi] + rh[...].astype(F32)
+    dproj_ref[...] = w_ref[...] + rh[...].astype(F32)
     for c in sent:
         c.wait_send()
     for end in closing:
         end()
+
+
+def put_out(*refs):
+    sem = refs[-1]
+    copies = [pltpu.make_async_copy(refs[i], refs[5 + i], sem.at[i]) for i in range(5)]
+    for c in copies:
+        c.start()
+    for c in copies:
+        c.wait()
 
 
 def per_device(queries, key_tokens, value_tokens, output_gradient, summary_proj, partner_bits):
@@ -537,9 +583,11 @@
             pltpu.VMEM((BLOCK, DIM), BF16),
             pltpu.VMEM((16, BLOCK), F32),
         ),
-        in_specs=[smem] + [vmem] * 5,
+        in_specs=[smem] + [pl.BlockSpec(memory_space=pl.ANY)] * 5,
         out_specs=[vmem] * 5,
         scratch_shapes=[
+            V((ROWS, DIM), BF16), V((BLOCK, DIM), BF16), V((BLOCK, DIM), BF16),
+            V((ROWS, DIM), BF16), V((SUM, BLOCK), BF16), pltpu.SemaphoreType.DMA((5,)),
             V((DIM, ROWS), BF16), V((DIM, ROWS), BF16),
             V((4, 2, 64, DIM), F32), V((3, 2, 64, DIM), F32),
             V((2, 64, DIM), F32), V((7, 64, DIM), BF16),
@@ -549,6 +597,7 @@
             V((5, BLOCK, DIM), BF16), V((5, BLOCK, DIM), BF16),
             V((5 * BLOCK + SUM, ROWS), BF16),
             V((1, ROWS), F32), V((1, ROWS), F32), V((8, ROWS), F32),
+            V((1, ROWS), F32), V((1, ROWS), F32),
             V((DIM, ROWS), F32), V((DIM, ROWS), F32),
             V((BLOCK, DIM), F32), V((BLOCK, DIM), F32),
             V((BLOCK, DIM), F32), V((BLOCK, DIM), F32),
@@ -560,8 +609,8 @@
             V((4, 2, 64, DIM), BF16), V((3, 2, 64, DIM), BF16),
             V((2, 64, DIM), F32), V((7, 64, DIM), BF16),
             V((2, 64, DIM), BF16), V((2, 64, DIM), BF16), V((4, 2, 64, DIM), BF16),
-            V((4, 2, 2, 16, BLOCK), BF16), V((7, 2, 16, BLOCK), BF16),
-            V((2, 16, BLOCK), F32), V((16, BLOCK), BF16), V((16, BLOCK), BF16),
+            V((4, 2, 2, 16, BLOCK), BF16), V((7, 16, BLOCK), BF16), V((7, 16, BLOCK), BF16),
+            V((16, BLOCK), F32), V((16, BLOCK), BF16), V((16, BLOCK), BF16),
             pltpu.SemaphoreType.DMA((COPIES,)), pltpu.SemaphoreType.DMA((COPIES,)),
             pltpu.SemaphoreType.REGULAR((6,)), pltpu.SemaphoreType.REGULAR, pltpu.SemaphoreType.REGULAR,
         ],
@@ -576,6 +625,17 @@
         output_gradient.reshape(ROWS, DIM),
         summary_proj,
     )
+    anywhere = pl.BlockSpec(memory_space=pl.ANY)
+    held = (out, dq, dk, dv, dproj)
+    held = tuple(pltpu.with_memory_space_constraint(a, pltpu.VMEM) for a in held)
+    out, dq, dk, dv, dproj = pl.pallas_call(
+        put_out,
+        name="put_out",
+        out_shape=tuple(jax.ShapeDtypeStruct(a.shape, a.dtype) for a in held),
+        in_specs=[vmem] * 5,
+        out_specs=[anywhere] * 5,
+        scratch_shapes=[pltpu.SemaphoreType.DMA((5,))],
+    )(*held)
     return (
         out.reshape(queries.shape),
         dq.reshape(queries.shape),

time: 83.8 us -> 77.9 us (0.930)
  local copies, waits for them, and re-layouts: 3.33 us -> 0 us
  Pallas kernels: 79.7 us -> 77 us
    pallas_call x1, Pallas kernels: 79.7 us -> 76.1 us  [per_device(): pl.pallas_call(kernel, name='butterfly', out_shape=(pltpu.VMEM((ROWS, DIM...]
    unnamed x5 -> x0, local copies, waits for them, and re-layouts: 3.33 us -> none
    pallas_call x0 -> x1, Pallas kernels: none -> 0.92 us  [per_device(): pl.pallas_call(put_out, name='put_out', out_shape=tuple((jax.ShapeDtypeSt...]
where the time goes in v4:
time: 77.9 us; the launch traced here: 77.7 us
  Pallas kernels  77 us (99%)
    pallas_call x1, Pallas kernels, per_device(): pl.pallas_call(kernel, name='butterfly', out_shape=(pltpu.VMEM((ROWS, DIM...  76.1 us

profile of v4, /device:TPU:1, one launch (start us, length us, event | category | flops | bytes accessed | tf_op | source)
XLA Modules:
  0.0 77.7 jit_solution(16815599079213017385)
XLA Ops:
  0.6 76.1 %butterfly.1 = (bf16[1024,128]{1,0:T(8,128)(2,1)S(1)}, bf16[1024,128]{1,0:T(8,128)(2,1)S(1)}, bf16[512,128]{1,0:T(8,128)(2,1)S(1)}, bf16[512,128]{1,0:T(8,128)(2,1)S(1)}, f32[16,512]{1,0:T(8,128)S(1)}) custom-call(s32[1,4]{1,0:T(1,128)} %bits_ref.1, bf16[1024,128]{1,0:T(8,128)(2,1)} %bitcast.8, bf16[512,128]{1,0:T(8,128)(2,1)} %bitcast.10, ...), custom_call_target="tpu_custom_call" | custom-call | tf_op jit(solution)/shard_map/butterfly/pallas_call | solution.py:576
  76.8 0.9 %put_out.1 = (bf16[1024,128]{1,0:T(8,128)(2,1)}, bf16[1024,128]{1,0:T(8,128)(2,1)}, bf16[512,128]{1,0:T(8,128)(2,1)}, bf16[512,128]{1,0:T(8,128)(2,1)}, f32[16,512]{1,0:T(8,128)}) custom-call(bf16[1024,128]{1,0:T(8,128)(2,1)S(1)} %get-tuple-element.15.refs_0_, bf16[1024,128]{1,0:T(8,128)(2,1)S(1)} %get-tuple-element.16.refs_1_, ...), custom_call_target="tpu_custom_call" | custom-call | tf_op jit(solution)/shard_map/put_out/pallas_call | solution.py:631

commit v5 on v4

--- a/solution.py
+++ b/solution.py
@@ -57,7 +57,7 @@
     bits_ref, q_in, k_in, v_in, do_in, proj_in,
     out_ref, dq_ref, dk_ref, dv_ref, dproj_ref,
     q_ref, k_ref, v_ref, do_ref, proj_ref, load_sem,
-    qt, dot_t, part, rx, xsum, zin, half, zbuf, agx,
+    qt, dot_t, part, rx, xsum, zin, zbuf, agx,
     kx, vx, kz, vz, ks, vs, e_ref, m_ref, l_ref, mslot, rescale, delta_ref, acc, dqt,
     gka, gva, own_gk, own_gv, gslot_k, gslot_v, gk, gv, rgk, rgv, zsk, zsv, zrk, zrv,
     part2, rx2, xsum2, zin2, half2, zbuf2, agx2,
@@ -258,7 +258,7 @@
             r = my_z - 3
             total = sums[r]
             for j in range(7):
-                describe(buf.at[0], into.at[j], {"seq": flipped(seq, 1)}, sends[0], first + j).wait_recv()
+                describe(into.at[j], into.at[j], {"seq": flipped(seq, 1)}, sends[0], first + j).wait_recv()
                 total = total + into[j].astype(F32)
             buf[r] = total.astype(BF16)
             for j, m in enumerate(Z_MASKS):
@@ -346,9 +346,8 @@
     tell(2)
     wait_recv(xs)
     xsum[...] = part[my_x] + rx[0] + rx[1] + rx[2]
-    half[...] = xsum[...].astype(BF16)
     hear(2)
-    at_three = reduce_z(half, zin)
+    at_three = reduce_z(xsum, zin)
     go_v(2)
     wait_recv(f_x1)
     choose(0, ks, kx, kz)
@@ -383,16 +382,36 @@
     sv[...] = agx[2:4].reshape(SUM, DIM)
     forward(SUMMARY, SUM, sk, sv)
 
-    @pl.when(my_z == 0)
-    def _():
-        pl.semaphore_wait(edge_sem, 1)
-        for m in Z_MASKS:
-            pl.semaphore_signal(hi_sem, inc=1, device_id={"seq": seq + m}, device_id_type=MESH)
-
     go_k(5)
     choose(3, ks, kx, kz)
     scores(SLOT + 3, BLOCK, ks.at[3])
     l_ref[...] = 1.0 / l_ref[...]
+
+    def weights(row, n, cols):
+        base = row * BLOCK
+        factor = jnp.exp2((mslot[row : row + 1, cols] - m_ref[:, cols]) * EXP2_SCALE) * l_ref[:, cols]
+        return e_ref[base : base + n, cols].astype(F32) * factor
+
+    summary_gv = jnp.zeros((SUM, DIM), F32)
+    for c in range(ROWS // CHUNK):
+        cols = pl.ds(c * CHUNK, CHUNK)
+        summary_gv = summary_gv + dot(weights(SUMMARY, SUM, cols).astype(BF16), do_ref[cols, :])
+    part2[2:4] = summary_gv.astype(BF16).reshape(2, 2, 64, DIM)
+    x_ids = [next(ids) for _ in X_MASKS]
+
+    def part_to(j):
+        peer = flipped(seq, X_MASKS[j])
+        return describe(part2.at[lax.div(peer, 8)], rx2.at[j], {"seq": peer}, x_ids[j], x_ids[j])
+
+    def send_parts(values):
+        for j, m in enumerate(X_MASKS):
+            peer_x = lax.div(flipped(seq, m), 8)
+
+            @pl.when((peer_x >= 2) if values else (peer_x < 2))
+            def _():
+                part_to(j).start()
+
+    send_parts(True)
     go_v(5)
     choose(3, vs, vx, vz)
     mix(SLOT + 3, BLOCK, vs.at[3])
@@ -401,28 +420,29 @@
     delta_ref[...] = jnp.sum(attended * dot_t[...].astype(F32), axis=0, keepdims=True)
 
     def backward(row, n, k, v, gk_acc, gv_acc):
-        base = row * BLOCK
         gk_acc[...] = jnp.zeros_like(gk_acc)
-        gv_acc[...] = jnp.zeros_like(gv_acc)
+        if gv_acc is not None:
+            gv_acc[...] = jnp.zeros_like(gv_acc)
 
         def step(c, carry):
             cols = pl.ds(pl.multiple_of(c * CHUNK, CHUNK), CHUNK)
-            factor = jnp.exp2((mslot[row : row + 1, cols] - m_ref[:, cols]) * EXP2_SCALE) * l_ref[:, cols]
-            p = e_ref[base : base + n, cols].astype(F32) * factor
+            p = weights(row, n, cols)
             dp = dot(v[...], dot_t[:, cols])
             ds = (p * (dp - delta_ref[:, cols])).astype(BF16)
             dqt[:, cols] += dot_tn(k[...], ds)
             gk_acc[...] += dot(ds, q_ref[cols, :])
-            gv_acc[...] += dot(p.astype(BF16), do_ref[cols, :])
+            if gv_acc is not None:
+                gv_acc[...] += dot(p.astype(BF16), do_ref[cols, :])
             return carry
 
         lax.fori_loop(0, ROWS // CHUNK, step, 0)
 
-    half_k, half_v = gka.at[0:SUM], gva.at[0:SUM]
-    backward(SUMMARY, SUM, sk, sv, half_k, half_v)
+    half_k = gka.at[0:SUM]
+    backward(SUMMARY, SUM, sk, sv, half_k, None)
     part2[0:2] = (half_k[...] * SCALE).astype(BF16).reshape(2, 2, 64, DIM)
-    part2[2:4] = half_v[...].astype(BF16).reshape(2, 2, 64, DIM)
-    xs = scatter_x(part2, rx2)
+    send_parts(False)
+    xs = [part_to(j) for j in range(3)]
+    sent.extend(xs)
 
     def slot_back(i):
         backward(SLOT + i, BLOCK, ks.at[i], vs.at[i], gka, gva)
@@ -491,6 +511,13 @@
     r_x1 = [give_back(gk, rgk, 0, 0, 8)]
     prepare(1)
     gathered = share_z(at_three, xsum2, zin2, zbuf2)
+
+    @pl.when(my_z == 0)
+    def _():
+        pl.semaphore_wait(edge_sem, 1)
+        for m in Z_MASKS:
+            pl.semaphore_signal(hi_sem, inc=1, device_id={"seq": seq + m}, device_id_type=MESH)
+
     back_k(3)
     backward(OWN, BLOCK, k_ref, v_ref, own_gk, own_gv)
     back_v(3)
@@ -590,8 +617,8 @@
             V((ROWS, DIM), BF16), V((SUM, BLOCK), BF16), pltpu.SemaphoreType.DMA((5,)),
             V((DIM, ROWS), BF16), V((DIM, ROWS), BF16),
             V((4, 2, 64, DIM), F32), V((3, 2, 64, DIM), F32),
-            V((2, 64, DIM), F32), V((7, 64, DIM), BF16),
-            V((2, 64, DIM), BF16), V((2, 64, DIM), BF16), V((4, 2, 64, DIM), BF16),
+            V((2, 64, DIM), F32), V((7, 64, DIM), F32),
+            V((2, 64, DIM), BF16), V((4, 2, 64, DIM), BF16),
             V((2, BLOCK, DIM), BF16), V((2, BLOCK, DIM), BF16),
             V((2, 4, BLOCK, DIM), BF16), V((2, 4, BLOCK, DIM), BF16),
             V((5, BLOCK, DIM), BF16), V((5, BLOCK, DIM), BF16),

time: 77.9 us -> 78.1 us (level)
  no operation moved by 1% of the time
where the time goes in v5:
time: 78.1 us; the launch traced here: 77.2 us
  Pallas kernels  76.6 us (98%)
    pallas_call x1, Pallas kernels, per_device(): pl.pallas_call(kernel, name='butterfly', out_shape=(pltpu.VMEM((ROWS, DIM...  75.6 us

profile of v5, /device:TPU:1, one launch (start us, length us, event | category | flops | bytes accessed | tf_op | source)
XLA Modules:
  0.0 77.2 jit_solution(7222762967429141848)
XLA Ops:
  0.6 75.6 %butterfly.1 = (bf16[1024,128]{1,0:T(8,128)(2,1)S(1)}, bf16[1024,128]{1,0:T(8,128)(2,1)S(1)}, bf16[512,128]{1,0:T(8,128)(2,1)S(1)}, bf16[512,128]{1,0:T(8,128)(2,1)S(1)}, f32[16,512]{1,0:T(8,128)S(1)}) custom-call(s32[1,4]{1,0:T(1,128)} %bits_ref.1, bf16[1024,128]{1,0:T(8,128)(2,1)} %bitcast.8, bf16[512,128]{1,0:T(8,128)(2,1)} %bitcast.10, ...), custom_call_target="tpu_custom_call" | custom-call | tf_op jit(solution)/shard_map/butterfly/pallas_call | solution.py:603
  76.3 0.9 %put_out.1 = (bf16[1024,128]{1,0:T(8,128)(2,1)}, bf16[1024,128]{1,0:T(8,128)(2,1)}, bf16[512,128]{1,0:T(8,128)(2,1)}, bf16[512,128]{1,0:T(8,128)(2,1)}, f32[16,512]{1,0:T(8,128)}) custom-call(bf16[1024,128]{1,0:T(8,128)(2,1)S(1)} %get-tuple-element.15.refs_0_, bf16[1024,128]{1,0:T(8,128)(2,1)S(1)} %get-tuple-element.16.refs_1_, ...), custom_call_target="tpu_custom_call" | custom-call | tf_op jit(solution)/shard_map/put_out/pallas_call | solution.py:658
